TPU v7x, 512 devices: a whole 4x4x16 slice. The times are simulated.
512 devices in a mesh: people: 32 (over z, core), blocks: 16 (over x, y).
Axes of the slice: x: 4, y: 4, z: 16, core: 2. Of those that a mesh axis runs over, the one named last changes fastest.
Arguments:
- allele_amounts: bfloat16 [131072, 8192], P('people', 'blocks'), may hold values from 0 to 2
- outcome_matrix: bfloat16 [131072, 16], P('people'), may hold values from -6 to 6
- shrinkage_factors: float32 [5], replicated, may hold values from 0.05 to 2
Outputs:
- ridge_coef: float32 [8192, 80], P('blocks')
- level1_gram: float32 [16, 80, 80], P('blocks')
- level1_cross: float32 [16, 80], P('blocks')
All inputs are finite; a program needn't handle non-finite values.
Results may differ from a plain program's by a relative error of at most 0.002.
Values may be sent and summed in bfloat16 or wider, within the bound.
A program may use at most 64 MiB of HBM per device.

v0:
```python
import math

import jax
import jax.numpy as jnp
from jax import lax
from jax.sharding import PartitionSpec as P

VARS = 512
OUTCOME_TOTAL = 16
LAMBDA_GRID = 5
ITERS = 8


def polynomial_iterate(apply_gram, starting_response, shrinkage_vector, eigenvalue_ceiling):
    radius = eigenvalue_ceiling / 2.0
    middle = shrinkage_vector + radius
    center = middle / radius
    weight = 1.0 / center
    shrunk_estimate = jnp.zeros_like(starting_response)
    remain = starting_response
    heading = remain / middle
    for sweep in range(ITERS):
        shrunk_estimate = shrunk_estimate + heading
        if sweep < ITERS - 1:
            remain = remain - (apply_gram(heading) + shrinkage_vector * heading)
            weight_next = 1.0 / (2.0 * center - weight)
            heading = weight_next * weight * heading + 2.0 * weight_next / radius * remain
            weight = weight_next
    return shrunk_estimate


def per_device(allele_amounts, outcome_matrix, shrinkage_factors):
    resident_subjects = allele_amounts.shape[0]
    headcount = resident_subjects * lax.axis_size("people")
    col_sums = jnp.sum(allele_amounts, axis=0, dtype=jnp.float32)
    square_sums = jnp.sum(jnp.square(allele_amounts.astype(jnp.float32)), axis=0)
    trait_sums = jnp.sum(outcome_matrix, axis=0, dtype=jnp.float32)
    gram_part = lax.dot_general(
        allele_amounts, allele_amounts, (((0,), (0,)), ((), ())), preferred_element_type=jnp.float32
    )
    cross_part = lax.dot_general(
        allele_amounts, outcome_matrix, (((0,), (0,)), ((), ())), preferred_element_type=jnp.float32
    )
    full_shrinkage_list = jnp.tile(shrinkage_factors, OUTCOME_TOTAL)
    gram_sum, cross_sum, col_sums, square_sums, trait_sums = lax.psum(
        (gram_part, cross_part, col_sums, square_sums, trait_sums), "people"
    )
    average = col_sums / headcount
    spread = jnp.sqrt(square_sums / headcount - average * average + 1e-05)
    scaled_covariance = (gram_sum / headcount - jnp.outer(average, average)) / jnp.outer(
        spread, spread
    )
    target_vector = (
        math.sqrt(headcount)
        * (cross_sum / headcount - jnp.outer(average, trait_sums / headcount))
        / spread[:, None]
    )
    eigenvalue_ceiling = jnp.max(jnp.sum(jnp.abs(scaled_covariance), axis=1))

    def apply_full(heading):
        return jnp.dot(
            scaled_covariance,
            heading,
            precision=lax.Precision.HIGHEST,
            preferred_element_type=jnp.float32,
        )

    ridge_coef = polynomial_iterate(
        apply_full,
        jnp.repeat(target_vector, LAMBDA_GRID, axis=1),
        full_shrinkage_list,
        eigenvalue_ceiling,
    )
    scaled_coef = (ridge_coef / (spread[:, None] * math.sqrt(VARS))).astype(jnp.bfloat16)
    offset = jnp.dot(average, scaled_coef.astype(jnp.float32), precision=lax.Precision.HIGHEST)
    model_predicted_phenotypes = (
        jnp.dot(allele_amounts, scaled_coef, preferred_element_type=jnp.float32) - offset
    ).astype(jnp.bfloat16)
    reformed_array = model_predicted_phenotypes.reshape(
        resident_subjects, OUTCOME_TOTAL, 1, LAMBDA_GRID
    )
    reassembled = lax.all_to_all(reformed_array, "blocks", split_axis=1, concat_axis=2, tiled=True)
    resident_outcomes = reassembled.shape[1]
    layered_blocks = reassembled.reshape(
        resident_subjects, resident_outcomes, reassembled.shape[2] * LAMBDA_GRID
    )
    trait_values = lax.dynamic_slice_in_dim(
        outcome_matrix, lax.axis_index("blocks") * resident_outcomes, resident_outcomes, 1
    )
    gram_level = lax.dot_general(
        layered_blocks,
        layered_blocks,
        (((0,), (0,)), ((1,), (1,))),
        preferred_element_type=jnp.float32,
    )
    cross_level = lax.dot_general(
        layered_blocks,
        trait_values,
        (((0,), (0,)), ((1,), (1,))),
        preferred_element_type=jnp.float32,
    )
    gram_level, cross_level = lax.psum((gram_level, cross_level), "people")
    return (ridge_coef, gram_level / headcount, cross_level / math.sqrt(headcount))


def solution(mesh):
    return jax.shard_map(
        per_device,
        mesh=mesh,
        in_specs=(P("people", "blocks"), P("people", None), P()),
        out_specs=(P("blocks", None), P("blocks", None, None), P("blocks", None)),
        check_vma=False,
    )
```

profile of v0, /device:TPU:1, one launch (start us, length us, event | category | flops | bytes accessed | tf_op | source)
XLA Modules:
  0.0 366.3 jit_solution(9383255707446749647)
XLA Ops:
  7.2 0.0 all-reduce.4.cloned.1.call-start
  7.2 6.9 %fusion.31 = f32[512,512]{1,0:T(8,128)} fusion(bf16[4096,512]{1,0:T(8,128)(2,1)} %param.3), kind=kOutput, calls=%fused_computation.76 | convolution fusion | flops 2147483648 | bytes 5242880 | tf_op jit(solution)/shard_map/dot_general | solution.py:38
  14.1 0.0 copy-start.2
  14.1 0.0 all-reduce.4.cloned.1.call-update
  14.1 0.0 copy-start
  14.1 0.0 copy-start.3
  14.1 3.5 convert_reduce_fusion
  17.6 0.0 copy-done.2
  17.6 0.0 copy-done
  17.6 0.6 fusion.32
  18.3 0.2 convert_reduce_fusion.1
  18.4 97.1 %all-reduce.1 = (f32[512,16]{0,1:T(8,128)S(1)}, f32[512]{0:T(512)S(1)}, f32[512]{0:T(512)S(1)}, f32[16]{0:T(128)S(1)}) all-reduce(f32[512,16]{0,1:T(8,128)S(1)} %fusion.32, f32[512]{0:T(512)S(1)} %get-tuple-element.4, f32[512]{0:T(512)S(1)} %get-tuple-element.3, ...), channel_id=1, replica_groups=mesh['people'=32,'blocks'=16] {'people'}, use_global_device_ids=true, to_apply=%region_0.0 | all-reduce | flops 9232 | bytes 73856 | tf_op jit(solution)/shard_map/psum | solution.py:45
  115.5 0.0 copy-done.3
  115.5 0.1 tile.10
  115.6 0.1 multiply_divide_fusion.1
  115.7 114.4 %all-reduce.4.cloned.1.call-done = f32[512,512]{1,0:T(8,128)} async-done(((f32[512,512]{1,0:T(8,128)}), f32[512,512]{1,0:T(8,128)}) %all-reduce.4.cloned.1.call-update) | async-done | bytes 1048592 | tf_op jit(solution)/shard_map/psum | solution.py:45
  230.1 1.7 abs_reduce_fusion
  231.8 0.6 reduce_max.9
  233.1 1.2 fusion.12
  234.3 1.2 multiply_add_fusion.3
  235.5 1.1 fusion.10
  236.6 0.0 copy-start.1
  236.7 1.2 fusion.9
  237.8 1.2 fusion.8
  239.0 1.2 fusion.7
  240.2 1.9 divide_convert_fusion
  242.1 0.1 convolution_bitcast_fusion.1
  242.2 0.0 copy-done.1
  242.2 1.5 fusion.2
  243.7 1.3 reshape.126
  245.0 6.5 %all-to-all-start = ((bf16[4096,16,1,5]{0,3,2,1:T(8,128)(2,1)}), bf16[4096,16,1,5]{0,3,2,1:T(8,128)(2,1)S(1)}, u32[]{:S(2)}, u32[]{:S(2)}) async-start(bf16[4096,16,1,5]{0,3,2,1:T(8,128)(2,1)} %bitcast.3), calls=%async_computation | async-start | bytes 2097152 | tf_op jit(solution)/shard_map/all_to_all | solution.py:82
  251.5 15.0 %all-to-all-done = bf16[4096,16,1,5]{0,3,2,1:T(8,128)(2,1)S(1)} async-done(((bf16[4096,16,1,5]{0,3,2,1:T(8,128)(2,1)}), bf16[4096,16,1,5]{0,3,2,1:T(8,128)(2,1)S(1)}, u32[]{:S(2)}, u32[]{:S(2)}) %all-to-all-start) | async-done | bytes 655392 | tf_op jit(solution)/shard_map/all_to_all | solution.py:82
  266.5 0.3 reshape.127
  266.8 0.3 convolution_bitcast_fusion
  267.1 0.3 fusion.24
  267.4 90.9 %all-reduce = (f32[1,80,80]{2,1,0:T(8,128)S(1)}, f32[1,80]{1,0:T(1,128)S(1)}) all-reduce(f32[1,80,80]{2,1,0:T(8,128)S(1)} %convolution_bitcast_fusion, f32[1,80]{1,0:T(1,128)S(1)} %fusion.24), channel_id=1, replica_groups=mesh['people'=32,'blocks'=16] {'people'}, use_global_device_ids=true, to_apply=%region_10.0 | all-reduce | flops 6480 | bytes 51840 | tf_op jit(solution)/shard_map/psum | solution.py:102
  358.3 0.6 broadcast_multiply_fusion
  358.9 0.5 broadcast_multiply_fusion.2
  (8 shorter events, 0.1 us)
Async XLA Ops:
  7.2 223.0 %all-reduce.4.cloned.1.call-start = ((), (), s32[]{:S(2)}) async-start(), calls=%async_computation.1 | async-start | bytes 2097152 | tf_op jit(solution)/shard_map/psum | solution.py:45
  14.1 3.5 copy-start.2
  14.1 3.5 copy-start
  14.1 101.4 %copy-start.3 = (f32[5]{0:T(128)S(1)}, f32[5]{0:T(128)}, u32[]{:S(2)}) copy-start(f32[5]{0:T(128)} %param.5) | copy-start | bytes 64
  236.6 5.6 %copy-start.1 = (bf16[4096,512]{1,0:T(8,128)(2,1)S(1)}, bf16[4096,512]{1,0:T(8,128)(2,1)}, u32[]{:S(2)}) copy-start(bf16[4096,512]{1,0:T(8,128)(2,1)} %param.3) | copy-start | bytes 12582916
  245.0 21.5 %all-to-all-start = ((bf16[4096,16,1,5]{0,3,2,1:T(8,128)(2,1)}), bf16[4096,16,1,5]{0,3,2,1:T(8,128)(2,1)S(1)}, u32[]{:S(2)}, u32[]{:S(2)}) async-start(bf16[4096,16,1,5]{0,3,2,1:T(8,128)(2,1)} %bitcast.3), calls=%async_computation | async-start | bytes 2097152 | tf_op jit(solution)/shard_map/all_to_all | solution.py:82
Sparse Core Ops, SparseCore 0:
  14.2 215.8 all-reduce.3
where the time goes:
time: 368 us; the launch traced here: 366 us
  blocking collectives  188 us (51%)
  waiting for transfers between devices  129 us (35%)
  matrix products  18.6 us (5%)
  between operations  14.8 us (4%)
  other arithmetic  7.19 us (2%)
  starting transfers between devices  6.57 us (2%)
    psum x1, waiting for transfers between devices, per_device(): lax.psum((gram_part, cross_part, col_sums, square_sums, trait_sums), 'peo...  114 us
    psum x1, blocking collectives, per_device(): lax.psum((gram_part, cross_part, col_sums, square_sums, trait_sums), 'peo...  97.1 us
    psum x1, blocking collectives, per_device(): gram_level, cross_level = lax.psum((gram_level, cross_level), 'people')  90.9 us
    all_to_all x1, waiting for transfers between devices, per_device(): lax.all_to_all(reformed_array, 'blocks', split_axis=1, concat_axis=2, til...  15 us
    dot_general x7, matrix products, apply_full(): jnp.dot(scaled_covariance, heading, precision=lax.Precision.HIGHEST, pref...  8.96 us
  transfers between devices with their start and end apart: 2, of which 2 were waited for; matrix products, arithmetic and copies ran while one was open for 1% of the time, Pallas kernels for 0%

commit v1 on v0

v1 whole, which is shorter than its diff:
```python
import functools
import math

import jax
import jax.numpy as jnp
from jax import lax
from jax.experimental import pallas as pl
from jax.experimental.pallas import tpu as pltpu
from jax.sharding import PartitionSpec as P

VARS = 512
TRAITS = 16
LAMBDAS = 5
ITERS = 8
SLOT = 8
PARTS = 16
MESH = pl.DeviceIdType.MESH
F32 = jnp.float32
BF16 = jnp.bfloat16
HIGHEST = lax.Precision.HIGHEST

TILE = 128
TILES = [(i, j) for i in range(VARS // TILE) for j in range(i, VARS // TILE)]
CROSS_AT = len(TILES) * TILE
SUMS_AT = CROSS_AT + TRAITS * (VARS // TILE)
TRAIT_AT = SUMS_AT + VARS // TILE
USED = SUMS_AT + 8
CONTRACT_ROWS = (((0,), (0,)), ((), ()))
CONTRACT_LANES = (((1,), (1,)), ((), ()))


def piece_rows(chips):
    return -(-USED // (2 * chips * 8)) * 8


def iota(shape, dim):
    return lax.broadcasted_iota(jnp.int32, shape, dim)


def far_first(n):
    return sorted(range(1, n), key=lambda d: -min(d, n - d))


def near_first(n):
    return sorted(range(1, n), key=lambda d: min(d, n - d))


def partial_kernel(x_ref, y_ref, out_ref, top, low, cross, sums, trait):
    step = pl.program_id(0)

    @pl.when(step == 0)
    def _():
        top[...] = jnp.zeros_like(top)
        low[...] = jnp.zeros_like(low)
        cross[...] = jnp.zeros_like(cross)
        sums[...] = jnp.zeros_like(sums)
        trait[...] = jnp.zeros_like(trait)

    half = VARS // 2
    x = x_ref[...]
    y = y_ref[...]
    top[...] += lax.dot_general(x[:, :half], x, CONTRACT_ROWS, preferred_element_type=F32)
    low[...] += lax.dot_general(
        x[:, half:], x[:, half:], CONTRACT_ROWS, preferred_element_type=F32
    )
    cross[...] += lax.dot_general(y, x, CONTRACT_ROWS, preferred_element_type=F32)
    sums[...] += jnp.dot(jnp.ones((8, x.shape[0]), BF16), x, preferred_element_type=F32)
    trait[...] += jnp.sum(y.astype(F32), axis=0, keepdims=True)

    @pl.when(step == pl.num_programs(0) - 1)
    def _():
        for at, (i, j) in enumerate(TILES):
            rows = slice(at * TILE, (at + 1) * TILE)
            if i * TILE < half:
                out_ref[rows, :] = top[i * TILE:(i + 1) * TILE, j * TILE:(j + 1) * TILE]
            else:
                a, b = i * TILE - half, j * TILE - half
                out_ref[rows, :] = low[a:a + TILE, b:b + TILE]
        for j in range(VARS // TILE):
            at = CROSS_AT + j * TRAITS
            out_ref[at:at + TRAITS, :] = cross[:, j * TILE:(j + 1) * TILE]
        out_ref[SUMS_AT:, :] = jnp.zeros((out_ref.shape[0] - SUMS_AT, TILE), F32)
        for j in range(VARS // TILE):
            out_ref[SUMS_AT + j:SUMS_AT + j + 1, :] = sums[0:1, j * TILE:(j + 1) * TILE]
        out_ref[TRAIT_AT:TRAIT_AT + 1, 0:TRAITS] = trait[...]


def position():
    person = lax.axis_index("people")
    return lax.div(person, 2), lax.rem(person, 2), lax.axis_index("blocks")


def remote(src, dst, send, recv, people, block):
    return pltpu.make_async_remote_copy(
        src_ref=src, dst_ref=dst, send_sem=send, recv_sem=recv,
        device_id=(people, block), device_id_type=MESH,
    )


def signal(people, block):
    pl.semaphore_signal(
        pltpu.get_barrier_semaphore(), inc=1, device_id=(people, block), device_id_type=MESH
    )


def people_sum_kernel(
    chips, in_ref, out_ref, half, mine, slots, full,
    pair_send, pair_recv, spread_send, spread_recv, gather_send, gather_recv, pass_send, pass_recv,
):
    z, c, b = position()
    other = 1 - c
    piece = slots.shape[1]
    rows = chips * piece
    signal(2 * z + other, b)
    for d in range(1, chips):
        signal(2 * lax.rem(z + d, chips) + c, b)
    pl.semaphore_wait(pltpu.get_barrier_semaphore(), chips)

    def own(core, chip):
        return pl.ds(pl.multiple_of(core * rows + chip * piece, 8), piece)

    pair = remote(
        in_ref.at[pl.ds(pl.multiple_of(other * rows, 8), rows)], half,
        pair_send, pair_recv, 2 * z + other, b,
    )
    pair.start()
    pair.wait()
    mine[...] = in_ref[pl.ds(pl.multiple_of(c * rows, 8), rows), :] + half[...]
    spread = {}
    for d in far_first(chips):
        to = lax.rem(z + d, chips)
        spread[d] = remote(
            mine.at[pl.ds(pl.multiple_of(to * piece, 8), piece)], slots.at[d],
            spread_send.at[d], spread_recv.at[d], 2 * to + c, b,
        )
        spread[d].start()
    total = mine[pl.ds(pl.multiple_of(z * piece, 8), piece), :]
    for d in near_first(chips):
        spread[d].wait_recv()
        total = total + slots[d]
    full[own(c, z), :] = total
    gather, passed = {}, {}
    for d in far_first(chips):
        gather[d] = remote(
            full.at[own(c, z)], full.at[own(c, z)],
            gather_send.at[d], gather_recv.at[d], 2 * lax.rem(z + d, chips) + c, b,
        )
        gather[d].start()
    for d in [0] + near_first(chips):
        if d:
            gather[d].wait_recv()
        here = own(c, lax.rem(z + chips - d, chips))
        passed[d] = remote(
            full.at[here], full.at[here], pass_send.at[d], pass_recv.at[d], 2 * z + other, b
        )
        passed[d].start()
    for d in [0] + near_first(chips):
        passed[d].wait()
        if d:
            spread[d].wait_send()
            gather[d].wait_send()
    out_ref[...] = full[...]


def chebyshev_mix(rows, per_trait, count, factors, radius):
    shape = (rows, ITERS * TRAITS)
    row = iota(shape, 0)
    lane = iota(shape, 1)
    if per_trait == 8:
        trait = lax.shift_right_logical(row, 3)
    else:
        trait = lax.shift_right_logical(row * 205, 10)
    which = row - trait * per_trait
    degree = lax.shift_right_logical(lane, 4)
    keep = (lane - degree * TRAITS == trait) & (which < LAMBDAS) & (row < count)
    lam = jnp.zeros(shape, F32) + factors[LAMBDAS - 1]
    for k in range(LAMBDAS - 1):
        lam = jnp.where(which == k, factors[k], lam)
    middle = lam + radius
    center = middle / radius
    weight = 1.0 / center
    left = jnp.ones(shape, F32)
    heading = jnp.where(degree == 0, 1.0 / middle, 0.0)
    total = heading
    for sweep in range(1, ITERS):
        left = left * weight
        weight_next = 1.0 / (2.0 * center - weight)
        heading = weight_next * weight * heading + jnp.where(
            degree == sweep, 2.0 * weight_next / radius * left, 0.0
        )
        weight = weight_next
        total = total + heading
    return jnp.where(keep, total, 0.0)


def solve_kernel(
    headcount, full, factors_ref, x_hbm, ridge_ref, pred_ref,
    xs, gram, high, low, basis, rows_scr, x_sem,
):
    load = pltpu.make_async_copy(x_hbm, xs, x_sem)
    load.start()
    for at, (i, j) in enumerate(TILES):
        tile = full[at * TILE:(at + 1) * TILE, :]
        gram[i * TILE:(i + 1) * TILE, j * TILE:(j + 1) * TILE] = tile
        if i != j:
            gram[j * TILE:(j + 1) * TILE, i * TILE:(i + 1) * TILE] = tile.T
    shape = (VARS, VARS)
    eye = iota(shape, 0) == iota(shape, 1)
    parts = range(VARS // TILE)
    average = jnp.concatenate(
        [full[SUMS_AT + j:SUMS_AT + j + 1, :] for j in parts], axis=1
    ) / headcount
    average_col = jnp.sum(
        jnp.where(eye, jnp.broadcast_to(average, shape), 0.0), axis=1, keepdims=True
    )
    diagonal = jnp.where(eye, gram[...], 0.0)
    square = jnp.sum(diagonal, axis=0, keepdims=True)
    square_col = jnp.sum(diagonal, axis=1, keepdims=True)
    inverse = 1.0 / jnp.sqrt(square / headcount - average * average + 1e-05)
    inverse_col = 1.0 / jnp.sqrt(square_col / headcount - average_col * average_col + 1e-05)
    standard = (gram[...] * (1.0 / headcount) - average_col * average) * (inverse_col * inverse)
    limit = jnp.max(jnp.sum(jnp.abs(standard), axis=0, keepdims=True), axis=1, keepdims=True)
    radius = limit / 2.0
    scaled = standard * (1.0 / radius)
    first = scaled.astype(BF16)
    high[...] = first
    low[...] = (scaled - first.astype(F32)).astype(BF16)

    cross = jnp.concatenate(
        [full[CROSS_AT + j * TRAITS:CROSS_AT + (j + 1) * TRAITS, :] for j in parts], axis=1
    )
    small = (TRAITS, TILE)
    trait_col = jnp.sum(
        jnp.where(
            iota(small, 0) == iota(small, 1),
            jnp.broadcast_to(full[TRAIT_AT:TRAIT_AT + 1, :], small), 0.0,
        ),
        axis=1, keepdims=True,
    )
    response = math.sqrt(headcount) * (
        cross / headcount - average * (trait_col / headcount)
    ) * inverse

    def apply(u):
        u_high = u.astype(BF16)
        u_low = (u - u_high.astype(F32)).astype(BF16)
        both = jnp.dot(
            jnp.concatenate([u_high, u_low], axis=0), high[...], preferred_element_type=F32
        )
        return both[:TRAITS] + (
            both[TRAITS:] + jnp.dot(u_high, low[...], preferred_element_type=F32)
        )

    before, now = None, response
    basis[0:TRAITS, :] = now
    for degree in range(1, ITERS):
        step = now - apply(now)
        before, now = now, step if before is None else 2.0 * step - before
        basis[degree * TRAITS:(degree + 1) * TRAITS, :] = now

    factors = [factors_ref[k] for k in range(LAMBDAS)]
    mix = chebyshev_mix(TRAITS * SLOT, SLOT, TRAITS * SLOT, factors, radius)
    solution_rows = jnp.dot(mix, basis[...], precision=HIGHEST, preferred_element_type=F32)
    coef = (solution_rows * (inverse * (1.0 / math.sqrt(VARS)))).astype(BF16)
    offset = jnp.sum(coef.astype(F32) * average, axis=1, keepdims=True)

    count = TRAITS * LAMBDAS
    mix = chebyshev_mix(TILE, LAMBDAS, count, factors, radius)
    packed = jnp.dot(mix, basis[...], precision=HIGHEST, preferred_element_type=F32)
    ridge_ref[...] = packed.T[:, :count]

    load.wait()
    width = xs.shape[0] // PARTS
    for part in range(PARTS):
        predicted = lax.dot_general(
            coef, xs[part * width:(part + 1) * width, :], CONTRACT_LANES,
            preferred_element_type=F32,
        ) - offset
        for t in range(TRAITS):
            rows_scr[t, part * LAMBDAS:(part + 1) * LAMBDAS, :] = predicted[
                t * SLOT:t * SLOT + LAMBDAS, :
            ]
    for t in range(TRAITS):
        pred_ref[t] = rows_scr[t].astype(BF16)


def slot_of(compact):
    block = lax.shift_right_logical(compact * 205, 10)
    return block * SLOT + (compact - block * LAMBDAS)


def level_one_kernel(
    chips, blocks, headcount, pred_ref, y_ref, gram_ref, cross_ref,
    recv, stacked, packed, half, mine, slots, final,
    move_send, move_recv, pair_send, pair_recv, spread_send, spread_recv, pass_send, pass_recv,
):
    z, c, b = position()
    person = 2 * z + c
    other = 1 - c
    for d in range(1, blocks):
        signal(person, lax.rem(b + d, blocks))
    signal(2 * z + other, b)
    for d in range(1, chips):
        signal(2 * lax.rem(z + d, chips) + c, b)

    stacked[...] = jnp.zeros_like(stacked)
    pick = (
        (iota((SLOT, TRAITS), 0) == LAMBDAS) & (iota((SLOT, TRAITS), 1) == b)
    ).astype(F32).astype(BF16)
    trait_row = lax.dot_general(
        pick, y_ref[...], CONTRACT_LANES, preferred_element_type=F32
    )
    pl.semaphore_wait(pltpu.get_barrier_semaphore(), blocks + chips - 1)

    moves = {}
    for d in range(1, blocks):
        to = lax.rem(b + d, blocks)
        moves[d] = remote(
            pred_ref.at[to], recv.at[d], move_send.at[d], move_recv.at[d], person, to
        )
        moves[d].start()
    width = recv.shape[2]

    def place(block, values):
        values = values.astype(F32)
        at = pl.ds(pl.multiple_of(block * SLOT, SLOT), LAMBDAS)
        for part in range(PARTS):
            stacked[at, part * width:(part + 1) * width] = values[
                part * LAMBDAS:(part + 1) * LAMBDAS, :
            ]

    place(b, pred_ref[b])
    for d in range(1, blocks):
        moves[d].wait_recv()
        place(lax.rem(b + blocks - d, blocks), recv[d])
    stacked[LAMBDAS:LAMBDAS + 1, :] = trait_row[LAMBDAS:LAMBDAS + 1, :]

    w = stacked[...].astype(BF16)
    gram = lax.dot_general(w, w, CONTRACT_LANES, preferred_element_type=F32)

    size = blocks * LAMBDAS
    part = size // 2
    square = (TILE, TILE)
    row, lane = iota(square, 0), iota(square, 1)
    cols_a = ((lane < size) & (row == slot_of(lane))) | ((lane == 120) & (row == LAMBDAS))
    cols_b = (
        (lane >= size) & (lane < size + part) & (row == slot_of(lane - part))
    ) | ((lane == 121) & (row == LAMBDAS))
    strip = (packed.shape[0], TILE)
    row, lane = iota(strip, 0), iota(strip, 1)
    rows_a = (row < part) & (lane == slot_of(row))
    rows_b = (row < part) & (lane == slot_of(row + part))

    def select(left, right):
        inner = jnp.dot(
            gram, right.astype(F32), precision=HIGHEST, preferred_element_type=F32
        )
        return jnp.dot(
            left.astype(F32), inner, precision=HIGHEST, preferred_element_type=F32
        )

    packed[...] = select(rows_a, cols_a) + select(rows_b, cols_b)

    rows = packed.shape[0] // 2

    def side(core):
        return pl.ds(pl.multiple_of(core * rows, 8), rows)

    pair = remote(packed.at[side(other)], half, pair_send, pair_recv, 2 * z + other, b)
    pair.start()
    pair.wait()
    mine[...] = packed[side(c), :] + half[...]
    spread = {}
    for d in far_first(chips):
        spread[d] = remote(
            mine, slots.at[z], spread_send.at[d], spread_recv.at[d],
            2 * lax.rem(z + d, chips) + c, b,
        )
        spread[d].start()
    slots[z] = mine[...]
    for d in near_first(chips):
        spread[d].wait_recv()
    total = slots[0]
    for chip in range(1, chips):
        total = total + slots[chip]
    final[side(c), :] = total
    passed = remote(final.at[side(c)], final.at[side(c)], pass_send, pass_recv, 2 * z + other, b)
    passed.start()
    passed.wait()
    for d in range(1, chips):
        spread[d].wait_send()
    for d in range(1, blocks):
        moves[d].wait_send()

    flat = final[...]
    turned = jnp.concatenate(
        [flat, jnp.zeros((TILE - flat.shape[0], TILE), F32)], axis=0
    ).T
    shifted = pltpu.roll(flat, TILE - part, 1)
    lane = iota((part, TILE), 1)
    lower = jnp.where(lane < part, turned[part:size, :], shifted[:part, :])
    gram_ref[0, 0:part, :] = flat[:part, :size] * (1.0 / headcount)
    gram_ref[0, part:size, :] = lower[:, :size] * (1.0 / headcount)
    lane = iota((1, TILE), 1)
    pair_row = jnp.where(lane < part, turned[120:121, :], pltpu.roll(turned[121:122, :], part, 1))
    cross_ref[...] = pair_row[:, :size] * (1.0 / math.sqrt(headcount))


VMEM = pl.BlockSpec(memory_space=pltpu.VMEM)
DMA = pltpu.SemaphoreType.DMA


def per_device(chips, blocks, x, y, factors):
    people = x.shape[0]
    headcount = float(people * chips * 2)
    piece = piece_rows(chips)
    total_rows = 2 * chips * piece
    tile = people // 8
    half = VARS // 2
    partial = pl.pallas_call(
        partial_kernel,
        grid=(people // tile,),
        in_specs=[
            pl.BlockSpec((tile, VARS), lambda i: (i, 0)),
            pl.BlockSpec((tile, TRAITS), lambda i: (i, 0)),
        ],
        out_specs=pl.BlockSpec((total_rows, TILE), lambda i: (0, 0)),
        out_shape=jax.ShapeDtypeStruct((total_rows, TILE), F32),
        scratch_shapes=[
            pltpu.VMEM((half, VARS), F32),
            pltpu.VMEM((half, half), F32),
            pltpu.VMEM((TRAITS, VARS), F32),
            pltpu.VMEM((8, VARS), F32),
            pltpu.VMEM((1, TRAITS), F32),
        ],
        name="partial_sums",
    )(x, y)
    summed = pl.pallas_call(
        functools.partial(people_sum_kernel, chips),
        in_specs=[VMEM],
        out_specs=VMEM,
        out_shape=jax.ShapeDtypeStruct((total_rows, TILE), F32),
        scratch_shapes=[
            pltpu.VMEM((total_rows // 2, TILE), F32),
            pltpu.VMEM((total_rows // 2, TILE), F32),
            pltpu.VMEM((chips, piece, TILE), F32),
            pltpu.VMEM((total_rows, TILE), F32),
            DMA, DMA, DMA((chips,)), DMA((chips,)), DMA((chips,)), DMA((chips,)),
            DMA((chips,)), DMA((chips,)),
        ],
        compiler_params=pltpu.CompilerParams(collective_id=0, has_side_effects=True),
        name="people_sum",
    )(partial)
    width = people // PARTS
    ridge, pred = pl.pallas_call(
        functools.partial(solve_kernel, headcount),
        in_specs=[
            VMEM,
            pl.BlockSpec(memory_space=pltpu.SMEM),
            pl.BlockSpec(memory_space=pl.ANY),
        ],
        out_specs=[VMEM, VMEM],
        out_shape=[
            jax.ShapeDtypeStruct((VARS, TRAITS * LAMBDAS), F32),
            jax.ShapeDtypeStruct((TRAITS, PARTS * LAMBDAS, width), BF16),
        ],
        scratch_shapes=[
            pltpu.VMEM((people, VARS), BF16),
            pltpu.VMEM((VARS, VARS), F32),
            pltpu.VMEM((VARS, VARS), BF16),
            pltpu.VMEM((VARS, VARS), BF16),
            pltpu.VMEM((ITERS * TRAITS, VARS), F32),
            pltpu.VMEM((TRAITS, PARTS * LAMBDAS, width), F32),
            DMA,
        ],
        name="solve",
    )(summed, factors, x)
    size = blocks * LAMBDAS
    rows = 48
    gram, cross = pl.pallas_call(
        functools.partial(level_one_kernel, chips, blocks, headcount),
        in_specs=[VMEM, VMEM],
        out_specs=[VMEM, VMEM],
        out_shape=[
            jax.ShapeDtypeStruct((1, size, size), F32),
            jax.ShapeDtypeStruct((1, size), F32),
        ],
        scratch_shapes=[
            pltpu.VMEM((blocks, PARTS * LAMBDAS, width), BF16),
            pltpu.VMEM((blocks * SLOT, people), F32),
            pltpu.VMEM((rows, TILE), F32),
            pltpu.VMEM((rows // 2, TILE), F32),
            pltpu.VMEM((rows // 2, TILE), F32),
            pltpu.VMEM((chips, rows // 2, TILE), F32),
            pltpu.VMEM((rows, TILE), F32),
            DMA((blocks,)), DMA((blocks,)), DMA, DMA, DMA((chips,)), DMA((chips,)), DMA, DMA,
        ],
        compiler_params=pltpu.CompilerParams(collective_id=1, has_side_effects=True),
        name="level_one",
    )(pred, y)
    return ridge, gram, cross


def solution(mesh):
    chips = mesh.shape["people"] // 2
    return jax.shard_map(
        functools.partial(per_device, chips, mesh.shape["blocks"]),
        mesh=mesh,
        in_specs=(P("people", "blocks"), P("people", None), P()),
        out_specs=(P("blocks", None), P("blocks", None, None), P("blocks", None)),
        check_vma=False,
    )
```

time: 368 us -> 118 us (0.32)
  blocking collectives: 188 us -> 0 us
  waiting for transfers between devices: 129 us -> 0 us
  Pallas kernels: 0 us -> 110 us
  matrix products: 18.6 us -> 0 us
  between operations: 14.8 us -> 0.66 us
  other arithmetic: 7.19 us -> 0 us
  starting transfers between devices: 6.57 us -> 0 us
  local copies, waits for them, and re-layouts: 1.7 us -> 6.54 us
    psum x2 -> x0, blocking collectives: 188 us -> none  [the longest x1 97.1 us: per_device(): lax.psum((gram_part, cross_part, col_sums, square_sums, trait_sums), 'peo...]
    psum x1 -> x0, waiting for transfers between devices: 114 us -> none  [per_device(): lax.psum((gram_part, cross_part, col_sums, square_sums, trait_sums), 'peo...]
    pallas_call x0 -> x4, Pallas kernels: none -> 110 us  [the longest x1 59.5 us: per_device(): pl.pallas_call(functools.partial(people_sum_kernel, chips), in_specs=[VME...]
    dot_general x13 -> x0, matrix products: 18.6 us -> none  [the longest x7 8.96 us: apply_full(): jnp.dot(scaled_covariance, heading, precision=lax.Precision.HIGHEST, pref...]
    all_to_all x1 -> x0, waiting for transfers between devices: 15 us -> none  [per_device(): lax.all_to_all(reformed_array, 'blocks', split_axis=1, concat_axis=2, til...]
    all_to_all x1 -> x0, starting transfers between devices: 6.53 us -> none  [per_device(): lax.all_to_all(reformed_array, 'blocks', split_axis=1, concat_axis=2, til...]
    unnamed x8 -> x4, local copies, waits for them, and re-layouts: 0.02 us -> 6.54 us
    reduce_sum x3 -> x0, other arithmetic: 5.3 us -> none  [the longest x1 3.48 us: per_device(): col_sums = jnp.sum(allele_amounts, axis=0, dtype=jnp.float32)]
  transfers between devices with their start and end apart: 2 -> 0, of which waited for: 2 -> 0; matrix products, arithmetic and copies ran while one was open for 1% -> 0% of each run, Pallas kernels for 0% -> 0%
where the time goes in v1:
time: 118 us; the launch traced here: 117 us
  Pallas kernels  110 us (93%)
  local copies, waits for them, and re-layouts  6.54 us (6%)
    pallas_call x1, Pallas kernels, per_device(): pl.pallas_call(functools.partial(people_sum_kernel, chips), in_specs=[VME...  59.5 us
    pallas_call x1, Pallas kernels, per_device(): pl.pallas_call(functools.partial(level_one_kernel, chips, blocks, headcou...  35.7 us
    pallas_call x1, Pallas kernels, per_device(): pl.pallas_call(partial_kernel, grid=(people // tile,), in_specs=[pl.Block...  7.97 us
    pallas_call x1, Pallas kernels, per_device(): pl.pallas_call(functools.partial(solve_kernel, headcount), in_specs=[VMEM...  6.66 us
    unnamed x4, local copies, waits for them, and re-layouts  6.54 us

profile of v1, /device:TPU:1, one launch (start us, length us, event | category | flops | bytes accessed | tf_op | source)
XLA Modules:
  0.0 117.1 jit_solution(15875295383986542310)
XLA Ops:
  0.6 2.2 %copy.6.y_ref = bf16[4096,16]{1,0:T(8,128)(2,1)} copy(bf16[4096,16]{0,1:T(8,128)(2,1)} %param.4) | data formatting | bytes 262144 | tf_op args[1]
  2.9 8.0 %partial_sums.1.in_ref = f32[1536,128]{1,0:T(8,128)} custom-call(bf16[4096,512]{1,0:T(8,128)(2,1)} %x_hbm.1, bf16[4096,16]{1,0:T(8,128)(2,1)} %copy.6.y_ref), custom_call_target="tpu_custom_call" | custom-call | tf_op jit(solution)/shard_map/partial_sums/pallas_call | solution.py:420
  10.8 59.5 %people_sum.1.full = f32[1536,128]{1,0:T(8,128)} custom-call(f32[1536,128]{1,0:T(8,128)} %partial_sums.1.in_ref), custom_call_target="tpu_custom_call" | custom-call | tf_op jit(solution)/shard_map/people_sum/pallas_call | solution.py:438
  70.4 6.7 %solve.1 = (f32[512,80]{1,0:T(8,128)}, bf16[16,80,256]{2,1,0:T(8,128)(2,1)}) custom-call(f32[1536,128]{1,0:T(8,128)} %people_sum.1.full, f32[5]{0:T(128)} %factors_ref.1, bf16[4096,512]{1,0:T(8,128)(2,1)} %x_hbm.1), custom_call_target="tpu_custom_call" | custom-call | tf_op jit(solution)/shard_map/solve/pallas_call | solution.py:455
  77.0 35.7 %level_one.1 = (f32[1,80,80]{2,1,0:T(8,128)}, f32[1,80]{1,0:T(1,128)}) custom-call(bf16[16,80,256]{2,1,0:T(8,128)(2,1)} %get-tuple-element.8.pred_ref, bf16[4096,16]{1,0:T(8,128)(2,1)} %copy.6.y_ref), custom_call_target="tpu_custom_call" | custom-call | tf_op jit(solution)/shard_map/level_one/pallas_call | solution.py:480
  112.8 1.7 %copy.8 = f32[512,80]{0,1:T(8,128)} copy(f32[512,80]{1,0:T(8,128)} %get-tuple-element.11) | data formatting | bytes 327680
  114.5 1.4 %copy.11 = f32[1,80,80]{2,1,0:T(8,128)} copy(f32[1,80,80]{2,1,0:T(8,128)} %get-tuple-element.18) | data formatting | bytes 51200
  115.9 1.2 %copy.12 = f32[1,80]{1,0:T(1,128)} copy(f32[1,80]{1,0:T(1,128)} %get-tuple-element.19) | data formatting | bytes 640

commit v2 on v1

v2 whole, which is shorter than its diff:
```python
import functools
import math

import jax
import jax.numpy as jnp
from jax import lax
from jax.experimental import pallas as pl
from jax.experimental.pallas import tpu as pltpu
from jax.sharding import PartitionSpec as P

VARS = 512
TRAITS = 16
LAMBDAS = 5
ITERS = 8
SLOT = 8
PARTS = 16
MESH = pl.DeviceIdType.MESH
F32 = jnp.float32
BF16 = jnp.bfloat16
HIGHEST = lax.Precision.HIGHEST

CHUNKS = 8
TILE = 128
EDGE = TILE // 2
STRIPS = VARS // TILE
OFF_TILES = [(i, j) for i in range(STRIPS) for j in range(i + 1, STRIPS)]
UPPER_AT = len(OFF_TILES) * TILE
LOWER_AT = UPPER_AT + STRIPS * EDGE
CROSS_AT = LOWER_AT + STRIPS // 2 * EDGE
SUMS_AT = CROSS_AT + TRAITS * STRIPS
TRAIT_AT = SUMS_AT + STRIPS
USED = SUMS_AT + 8
CONTRACT_ROWS = (((0,), (0,)), ((), ()))
CONTRACT_LANES = (((1,), (1,)), ((), ()))


def piece_rows(chips):
    return -(-USED // (2 * chips * 8)) * 8


def iota(shape, dim):
    return lax.broadcasted_iota(jnp.int32, shape, dim)


def far_first(n):
    return sorted(range(1, n), key=lambda d: -min(d, n - d))


def near_first(n):
    return sorted(range(1, n), key=lambda d: min(d, n - d))


def partial_sums(x_hbm, y_ref, xs, part, top, low, tail, x_sems):
    tile = xs.shape[0] // CHUNKS

    def chunk(i):
        return pl.ds(pl.multiple_of(i * tile, tile), tile)

    def load(i):
        return pltpu.make_async_copy(x_hbm.at[chunk(i)], xs.at[chunk(i)], x_sems.at[i])

    for i in range(CHUNKS):
        load(i).start()
    top[...] = jnp.zeros_like(top)
    low[...] = jnp.zeros_like(low)
    tail[...] = jnp.zeros_like(tail)
    half = VARS // 2

    def step(i, carry):
        load(i).wait()
        x = xs[chunk(i), :]
        lead = jnp.concatenate([y_ref[:, chunk(i)], jnp.ones((TRAITS, tile), BF16)], axis=0)
        top[...] += lax.dot_general(x[:, :half], x, CONTRACT_ROWS, preferred_element_type=F32)
        low[...] += lax.dot_general(
            x[:, half:], x[:, half:], CONTRACT_ROWS, preferred_element_type=F32
        )
        tail[...] += jnp.dot(lead, x, preferred_element_type=F32)
        return carry

    lax.fori_loop(0, CHUNKS, step, 0)

    def tile_of(i, j, first):
        rows, columns = i * TILE + first, j * TILE
        source = top
        if rows >= half:
            source, rows, columns = low, rows - half, columns - half
        return source[rows:(i + 1) * TILE - (half if source is low else 0), columns:columns + TILE]

    for at, (i, j) in enumerate(OFF_TILES):
        part[at * TILE:(at + 1) * TILE, :] = tile_of(i, j, 0)
    left = iota((EDGE, TILE), 1) < EDGE
    for i in range(STRIPS):
        at = UPPER_AT + i * EDGE
        part[at:at + EDGE, :] = tile_of(i, i, 0)[:EDGE]
    for i in range(STRIPS // 2):
        at = LOWER_AT + i * EDGE
        part[at:at + EDGE, :] = jnp.where(
            left, pltpu.roll(tile_of(2 * i, 2 * i, EDGE), EDGE, 1),
            tile_of(2 * i + 1, 2 * i + 1, EDGE),
        )
    for j in range(STRIPS):
        at = CROSS_AT + j * TRAITS
        part[at:at + TRAITS, :] = tail[0:TRAITS, j * TILE:(j + 1) * TILE]
    part[SUMS_AT:, :] = jnp.zeros((part.shape[0] - SUMS_AT, TILE), F32)
    for j in range(STRIPS):
        part[SUMS_AT + j:SUMS_AT + j + 1, :] = tail[
            TRAITS:TRAITS + 1, j * TILE:(j + 1) * TILE
        ]
    trait = jnp.sum(y_ref[...].astype(F32), axis=1, keepdims=True)
    small = (TRAITS, TILE)
    part[TRAIT_AT:TRAIT_AT + 1, :] = jnp.sum(
        jnp.where(iota(small, 0) == iota(small, 1), jnp.broadcast_to(trait, small), 0.0),
        axis=0, keepdims=True,
    )


def position():
    person = lax.axis_index("people")
    return lax.div(person, 2), lax.rem(person, 2), lax.axis_index("blocks")


def remote(src, dst, send, recv, people, block):
    return pltpu.make_async_remote_copy(
        src_ref=src, dst_ref=dst, send_sem=send, recv_sem=recv,
        device_id=(people, block), device_id_type=MESH,
    )


def signal(people, block):
    pl.semaphore_signal(
        pltpu.get_barrier_semaphore(), inc=1, device_id=(people, block), device_id_type=MESH
    )


def people_sum(chips, part, full, half, mine, other_half, ours, slots, sems):
    (
        pair_send, pair_recv, near_send, near_recv, spread_send, spread_recv,
        gather_send, gather_recv, near_back_send, near_back_recv, pass_send, pass_recv,
    ) = sems
    z, c, b = position()
    other = 1 - c
    odd, place = lax.rem(z, 2), lax.div(z, 2)
    peers = chips // 2
    near = lax.rem(z + (1 - 2 * odd) * (1 - 2 * c) + chips, chips)
    piece = slots.shape[1]
    rows = chips * piece
    side = peers * piece

    def rows_at(start, count):
        return pl.ds(pl.multiple_of(start, 8), count)

    pair = remote(
        part.at[rows_at(other * rows, rows)], half, pair_send, pair_recv, 2 * z + other, b
    )
    pair.start()
    pair.wait()
    mine[...] = part[rows_at(c * rows, rows), :] + half[...]
    swap = remote(
        mine.at[rows_at((1 - odd) * side, side)], other_half,
        near_send, near_recv, 2 * near + c, b,
    )
    swap.start()
    swap.wait()
    ours[...] = mine[rows_at(odd * side, side), :] + other_half[...]
    spread = {}
    for d in far_first(peers):
        to = lax.rem(place + d, peers)
        spread[d] = remote(
            ours.at[rows_at(to * piece, piece)], slots.at[d],
            spread_send.at[d], spread_recv.at[d], 2 * (2 * to + odd) + c, b,
        )
        spread[d].start()
    total = ours[rows_at(place * piece, piece), :]
    for d in near_first(peers):
        spread[d].wait_recv()
        total = total + slots[d]

    def own(parity, at):
        return rows_at(c * rows + parity * side + at * piece, piece)

    full[own(odd, place), :] = total
    here = own(odd, place)
    gather = {}
    for d in far_first(peers):
        to = 2 * (2 * lax.rem(place + d, peers) + odd) + c
        gather[d] = remote(
            full.at[here], full.at[here], gather_send.at[d], gather_recv.at[d], to, b
        )
        gather[d].start()
    back, passed = {}, {}
    for d in [0] + near_first(peers):
        if d:
            gather[d].wait_recv()
        here = own(odd, lax.rem(place + peers - d, peers))
        back[d] = remote(
            full.at[here], full.at[here], near_back_send.at[d], near_back_recv.at[d],
            2 * near + c, b,
        )
        back[d].start()
        passed[d] = remote(
            full.at[here], full.at[here], pass_send.at[d], pass_recv.at[d], 2 * z + other, b
        )
        passed[d].start()
    near_place = lax.div(near, 2)
    for d in [0] + near_first(peers):
        back[d].wait_recv()
        here = own(1 - odd, lax.rem(near_place + peers - d, peers))
        passed[peers + d] = remote(
            full.at[here], full.at[here], pass_send.at[peers + d], pass_recv.at[peers + d],
            2 * z + other, b,
        )
        passed[peers + d].start()
    for copy in passed.values():
        copy.wait()
    for d in range(peers):
        back[d].wait_send()
        if d:
            spread[d].wait_send()
            gather[d].wait_send()


def chebyshev_mix(rows, per_trait, count, factors, radius):
    shape = (rows, ITERS * TRAITS)
    row = iota(shape, 0)
    lane = iota(shape, 1)
    if per_trait == 8:
        trait = lax.shift_right_logical(row, 3)
    else:
        trait = lax.shift_right_logical(row * 205, 10)
    which = row - trait * per_trait
    degree = lax.shift_right_logical(lane, 4)
    keep = (lane - degree * TRAITS == trait) & (which < LAMBDAS) & (row < count)
    lam = jnp.zeros(shape, F32) + factors[LAMBDAS - 1]
    for k in range(LAMBDAS - 1):
        lam = jnp.where(which == k, factors[k], lam)
    middle = lam + radius
    center = middle / radius
    weight = 1.0 / center
    left = jnp.ones(shape, F32)
    heading = jnp.where(degree == 0, 1.0 / middle, 0.0)
    total = heading
    for sweep in range(1, ITERS):
        left = left * weight
        weight_next = 1.0 / (2.0 * center - weight)
        heading = weight_next * weight * heading + jnp.where(
            degree == sweep, 2.0 * weight_next / radius * left, 0.0
        )
        weight = weight_next
        total = total + heading
    return jnp.where(keep, total, 0.0)


def solve(headcount, full, factors_ref, xs, pred, gram, high, low, basis, rows_scr):
    for at, (i, j) in enumerate(OFF_TILES):
        tile = full[at * TILE:(at + 1) * TILE, :]
        gram[i * TILE:(i + 1) * TILE, j * TILE:(j + 1) * TILE] = tile
        gram[j * TILE:(j + 1) * TILE, i * TILE:(i + 1) * TILE] = tile.T
    left = iota((EDGE, TILE), 1) < EDGE
    for i in range(STRIPS):
        upper = full[UPPER_AT + i * EDGE:UPPER_AT + (i + 1) * EDGE, :]
        at = LOWER_AT + i // 2 * EDGE
        lower = full[at:at + EDGE, :]
        if i % 2 == 0:
            lower = pltpu.roll(lower, EDGE, 1)
        turned = jnp.concatenate([upper, jnp.zeros((EDGE, TILE), F32)], axis=0).T
        columns = slice(i * TILE, (i + 1) * TILE)
        gram[i * TILE:i * TILE + EDGE, columns] = upper
        gram[i * TILE + EDGE:(i + 1) * TILE, columns] = jnp.where(left, turned[EDGE:, :], lower)
    shape = (VARS, VARS)
    eye = iota(shape, 0) == iota(shape, 1)
    parts = range(VARS // TILE)
    average = jnp.concatenate(
        [full[SUMS_AT + j:SUMS_AT + j + 1, :] for j in parts], axis=1
    ) / headcount
    average_col = jnp.sum(
        jnp.where(eye, jnp.broadcast_to(average, shape), 0.0), axis=1, keepdims=True
    )
    diagonal = jnp.where(eye, gram[...], 0.0)
    square = jnp.sum(diagonal, axis=0, keepdims=True)
    square_col = jnp.sum(diagonal, axis=1, keepdims=True)
    inverse = 1.0 / jnp.sqrt(square / headcount - average * average + 1e-05)
    inverse_col = 1.0 / jnp.sqrt(square_col / headcount - average_col * average_col + 1e-05)
    standard = (gram[...] * (1.0 / headcount) - average_col * average) * (inverse_col * inverse)
    limit = jnp.max(jnp.sum(jnp.abs(standard), axis=0, keepdims=True), axis=1, keepdims=True)
    radius = limit / 2.0
    scaled = standard * (1.0 / radius)
    first = scaled.astype(BF16)
    high[...] = first
    low[...] = (scaled - first.astype(F32)).astype(BF16)

    cross = jnp.concatenate(
        [full[CROSS_AT + j * TRAITS:CROSS_AT + (j + 1) * TRAITS, :] for j in parts], axis=1
    )
    small = (TRAITS, TILE)
    trait_col = jnp.sum(
        jnp.where(
            iota(small, 0) == iota(small, 1),
            jnp.broadcast_to(full[TRAIT_AT:TRAIT_AT + 1, :], small), 0.0,
        ),
        axis=1, keepdims=True,
    )
    response = math.sqrt(headcount) * (
        cross / headcount - average * (trait_col / headcount)
    ) * inverse

    def apply(u):
        u_high = u.astype(BF16)
        u_low = (u - u_high.astype(F32)).astype(BF16)
        both = jnp.dot(
            jnp.concatenate([u_high, u_low], axis=0), high[...], preferred_element_type=F32
        )
        return both[:TRAITS] + (
            both[TRAITS:] + jnp.dot(u_high, low[...], preferred_element_type=F32)
        )

    before, now = None, response
    basis[0:TRAITS, :] = now
    for degree in range(1, ITERS):
        step = now - apply(now)
        before, now = now, step if before is None else 2.0 * step - before
        basis[degree * TRAITS:(degree + 1) * TRAITS, :] = now

    factors = [factors_ref[k] for k in range(LAMBDAS)]
    mix = chebyshev_mix(TRAITS * SLOT, SLOT, TRAITS * SLOT, factors, radius)
    solution_rows = jnp.dot(mix, basis[...], precision=HIGHEST, preferred_element_type=F32)
    coef = (solution_rows * (inverse * (1.0 / math.sqrt(VARS)))).astype(BF16)
    offset = jnp.sum(coef.astype(F32) * average, axis=1, keepdims=True)

    width = xs.shape[0] // PARTS
    for part in range(PARTS):
        predicted = lax.dot_general(
            coef, xs[part * width:(part + 1) * width, :], CONTRACT_LANES,
            preferred_element_type=F32,
        ) - offset
        for t in range(TRAITS):
            rows_scr[t, part * LAMBDAS:(part + 1) * LAMBDAS, :] = predicted[
                t * SLOT:t * SLOT + LAMBDAS, :
            ]
    for t in range(TRAITS):
        pred[t] = rows_scr[t].astype(BF16)
    return factors, radius


def slot_of(compact):
    block = lax.shift_right_logical(compact * 205, 10)
    return block * SLOT + (compact - block * LAMBDAS)


def whole_kernel(
    chips, blocks, headcount, y_ref, factors_ref, x_hbm, ridge_ref, final_ref,
    xs, part, top, low, tail, full, half, mine, other_half, ours, slots,
    gram_scr, high, low_part, basis, rows_scr, pred, recv, stacked,
    packed, last_half, last_mine, last_slots, final,
    x_sems, *sems,
):
    z, c, b = position()
    person = 2 * z + c
    other = 1 - c
    for d in range(1, chips):
        signal(2 * lax.rem(z + d, chips) + c, b)
    signal(2 * z + other, b)
    for d in range(1, blocks):
        signal(person, lax.rem(b + d, blocks))

    partial_sums(x_hbm, y_ref, xs, part, top, low, tail, x_sems)
    stacked[...] = jnp.zeros_like(stacked)
    pl.semaphore_wait(pltpu.get_barrier_semaphore(), blocks + chips - 1)
    people_sum(chips, part, full, half, mine, other_half, ours, slots, sems[:12])
    factors, radius = solve(
        headcount, full, factors_ref, xs, pred, gram_scr, high, low_part, basis, rows_scr
    )

    (
        move_send, move_recv, pair_send, pair_recv, spread_send, spread_recv, pass_send, pass_recv,
    ) = sems[12:]
    moves = {}
    for d in range(1, blocks):
        to = lax.rem(b + d, blocks)
        moves[d] = remote(
            pred.at[to], recv.at[d], move_send.at[d], move_recv.at[d], person, to
        )
        moves[d].start()

    count = TRAITS * LAMBDAS
    mix = chebyshev_mix(count, LAMBDAS, count, factors, radius)
    ridge_ref[...] = jnp.dot(mix, basis[...], precision=HIGHEST, preferred_element_type=F32)
    pick = (
        (iota((SLOT, TRAITS), 0) == LAMBDAS) & (iota((SLOT, TRAITS), 1) == b)
    ).astype(F32).astype(BF16)
    trait_row = jnp.dot(pick, y_ref[...], preferred_element_type=F32)
    width = recv.shape[2]

    def place(block, values):
        values = values.astype(F32)
        at = pl.ds(pl.multiple_of(block * SLOT, SLOT), LAMBDAS)
        for part in range(PARTS):
            stacked[at, part * width:(part + 1) * width] = values[
                part * LAMBDAS:(part + 1) * LAMBDAS, :
            ]

    place(b, pred[b])
    for d in range(1, blocks):
        moves[d].wait_recv()
        place(lax.rem(b + blocks - d, blocks), recv[d])
    stacked[LAMBDAS:LAMBDAS + 1, :] = trait_row[LAMBDAS:LAMBDAS + 1, :]

    w = stacked[...].astype(BF16)
    gram = lax.dot_general(w, w, CONTRACT_LANES, preferred_element_type=F32)

    size = blocks * LAMBDAS
    part = size // 2
    square = (TILE, TILE)
    row, lane = iota(square, 0), iota(square, 1)
    cols_a = ((lane < size) & (row == slot_of(lane))) | ((lane == 120) & (row == LAMBDAS))
    cols_b = (
        (lane >= size) & (lane < size + part) & (row == slot_of(lane - part))
    ) | ((lane == 121) & (row == LAMBDAS))
    strip = (packed.shape[0], TILE)
    row, lane = iota(strip, 0), iota(strip, 1)
    rows_a = (row < part) & (lane == slot_of(row))
    rows_b = (row < part) & (lane == slot_of(row + part))

    def select(left, right):
        inner = jnp.dot(
            gram, right.astype(F32), precision=HIGHEST, preferred_element_type=F32
        )
        return jnp.dot(
            left.astype(F32), inner, precision=HIGHEST, preferred_element_type=F32
        )

    packed[...] = select(rows_a, cols_a) + select(rows_b, cols_b)

    rows = packed.shape[0] // 2

    def side(core):
        return pl.ds(pl.multiple_of(core * rows, 8), rows)

    pair = remote(packed.at[side(other)], last_half, pair_send, pair_recv, 2 * z + other, b)
    pair.start()
    pair.wait()
    last_mine[...] = packed[side(c), :] + last_half[...]
    spread = {}
    for d in far_first(chips):
        spread[d] = remote(
            last_mine, last_slots.at[z], spread_send.at[d], spread_recv.at[d],
            2 * lax.rem(z + d, chips) + c, b,
        )
        spread[d].start()
    last_slots[z] = last_mine[...]
    for d in near_first(chips):
        spread[d].wait_recv()
    total = last_slots[0]
    for chip in range(1, chips):
        total = total + last_slots[chip]
    final[side(c), :] = total
    passed = remote(final.at[side(c)], final.at[side(c)], pass_send, pass_recv, 2 * z + other, b)
    passed.start()
    passed.wait()
    for d in range(1, chips):
        spread[d].wait_send()
    for d in range(1, blocks):
        moves[d].wait_send()

    final_ref[...] = final[...]


def finish_kernel(size, headcount, rows_ref, flat_ref, ridge_ref, gram_ref, cross_ref):
    ridge_ref[...] = rows_ref[...]
    part = size // 2
    flat = flat_ref[...]
    turned = jnp.concatenate(
        [flat, jnp.zeros((TILE - flat.shape[0], TILE), F32)], axis=0
    ).T
    shifted = pltpu.roll(flat, TILE - part, 1)
    lane = iota((part, TILE), 1)
    lower = jnp.where(lane < part, turned[part:size, :], shifted[:part, :])
    gram_ref[0, 0:part, :] = flat[:part, :size] * (1.0 / headcount)
    gram_ref[0, part:size, :] = lower[:, :size] * (1.0 / headcount)
    lane = iota((1, TILE), 1)
    pair_row = jnp.where(lane < part, turned[120:121, :], pltpu.roll(turned[121:122, :], part, 1))
    cross_ref[...] = pair_row[:, :size] * (1.0 / math.sqrt(headcount))


VMEM = pl.BlockSpec(memory_space=pltpu.VMEM)
DMA = pltpu.SemaphoreType.DMA


def per_device(chips, blocks, x, y, factors):
    people = x.shape[0]
    headcount = float(people * chips * 2)
    piece = piece_rows(chips)
    total_rows = 2 * chips * piece
    core_rows = chips * piece
    peers = chips // 2
    half = VARS // 2
    width = people // PARTS
    size = blocks * LAMBDAS
    rows = 48
    rows_shape = jax.ShapeDtypeStruct((TRAITS * LAMBDAS, VARS), F32)
    ridge, final = pl.pallas_call(
        functools.partial(whole_kernel, chips, blocks, headcount),
        in_specs=[
            VMEM,
            pl.BlockSpec(memory_space=pltpu.SMEM),
            pl.BlockSpec(memory_space=pl.ANY),
        ],
        out_specs=[VMEM, VMEM],
        out_shape=[rows_shape, jax.ShapeDtypeStruct((rows, TILE), F32)],
        scratch_shapes=[
            pltpu.VMEM((people, VARS), BF16),
            pltpu.VMEM((total_rows, TILE), F32),
            pltpu.VMEM((half, VARS), F32),
            pltpu.VMEM((half, half), F32),
            pltpu.VMEM((2 * TRAITS, VARS), F32),
            pltpu.VMEM((total_rows, TILE), F32),
            pltpu.VMEM((core_rows, TILE), F32),
            pltpu.VMEM((core_rows, TILE), F32),
            pltpu.VMEM((core_rows // 2, TILE), F32),
            pltpu.VMEM((core_rows // 2, TILE), F32),
            pltpu.VMEM((peers, piece, TILE), F32),
            pltpu.VMEM((VARS, VARS), F32),
            pltpu.VMEM((VARS, VARS), BF16),
            pltpu.VMEM((VARS, VARS), BF16),
            pltpu.VMEM((ITERS * TRAITS, VARS), F32),
            pltpu.VMEM((TRAITS, PARTS * LAMBDAS, width), F32),
            pltpu.VMEM((TRAITS, PARTS * LAMBDAS, width), BF16),
            pltpu.VMEM((blocks, PARTS * LAMBDAS, width), BF16),
            pltpu.VMEM((blocks * SLOT, people), F32),
            pltpu.VMEM((rows, TILE), F32),
            pltpu.VMEM((rows // 2, TILE), F32),
            pltpu.VMEM((rows // 2, TILE), F32),
            pltpu.VMEM((chips, rows // 2, TILE), F32),
            pltpu.VMEM((rows, TILE), F32),
            DMA((CHUNKS,)),
            DMA, DMA, DMA, DMA, DMA((peers,)), DMA((peers,)), DMA((peers,)), DMA((peers,)),
            DMA((peers,)), DMA((peers,)), DMA((chips,)), DMA((chips,)),
            DMA((blocks,)), DMA((blocks,)), DMA, DMA, DMA((chips,)), DMA((chips,)), DMA, DMA,
        ],
        compiler_params=pltpu.CompilerParams(collective_id=0, has_side_effects=True),
        name="whole",
    )(y.T, factors, x)
    ridge, gram, cross = pl.pallas_call(
        functools.partial(finish_kernel, size, headcount),
        in_specs=[VMEM, VMEM],
        out_specs=[VMEM, VMEM, VMEM],
        out_shape=[
            rows_shape,
            jax.ShapeDtypeStruct((1, size, size), F32),
            jax.ShapeDtypeStruct((1, size), F32),
        ],
        name="finish",
    )(ridge, final)
    return ridge.T, gram, cross


def solution(mesh):
    chips = mesh.shape["people"] // 2
    return jax.shard_map(
        functools.partial(per_device, chips, mesh.shape["blocks"]),
        mesh=mesh,
        in_specs=(P("people", "blocks"), P("people", None), P()),
        out_specs=(P("blocks", None), P("blocks", None, None), P("blocks", None)),
        check_vma=False,
    )
```

time: 118 us -> 82.8 us (0.70)
  Pallas kernels: 110 us -> 81.8 us
  local copies, waits for them, and re-layouts: 6.54 us -> 0 us
    pallas_call x4 -> x2, Pallas kernels: 110 us -> 81.8 us  [the longest x1 80.1 us: per_device(): pl.pallas_call(functools.partial(whole_kernel, chips, blocks, headcount),...]
    unnamed x4 -> x0, local copies, waits for them, and re-layouts: 6.54 us -> none
where the time goes in v2:
time: 82.8 us; the launch traced here: 82.5 us
  Pallas kernels  81.8 us (99%)
    pallas_call x1, Pallas kernels, per_device(): pl.pallas_call(functools.partial(whole_kernel, chips, blocks, headcount),...  80.1 us
    pallas_call x1, Pallas kernels, per_device(): pl.pallas_call(functools.partial(finish_kernel, size, headcount), in_spec...  1.69 us

profile of v2, /device:TPU:1, one launch (start us, length us, event | category | flops | bytes accessed | tf_op | source)
XLA Modules:
  0.0 82.5 jit_solution(1619147822123602258)
XLA Ops:
  0.6 80.1 %whole.1 = (f32[80,512]{1,0:T(8,128)}, f32[48,128]{1,0:T(8,128)}) custom-call(bf16[16,4096]{1,0:T(8,128)(2,1)} %bitcast.2, f32[5]{0:T(128)} %factors_ref.1, bf16[4096,512]{1,0:T(8,128)(2,1)} %x_hbm.1), custom_call_target="tpu_custom_call" | custom-call | tf_op jit(solution)/shard_map/whole/pallas_call | solution.py:500
  80.8 1.7 %finish.1 = (f32[80,512]{1,0:T(8,128)}, f32[1,80,80]{2,1,0:T(8,128)}, f32[1,80]{1,0:T(1,128)}) custom-call(f32[80,512]{1,0:T(8,128)} %get-tuple-element.8.rows_ref, f32[48,128]{1,0:T(8,128)} %get-tuple-element.9.flat_ref), custom_call_target="tpu_custom_call" | custom-call | tf_op jit(solution)/shard_map/finish/pallas_call | solution.py:542

commit v3 on v2

--- a/solution.py
+++ b/solution.py
@@ -23,21 +23,18 @@
 TILE = 128
 EDGE = TILE // 2
 STRIPS = VARS // TILE
-OFF_TILES = [(i, j) for i in range(STRIPS) for j in range(i + 1, STRIPS)]
-UPPER_AT = len(OFF_TILES) * TILE
-LOWER_AT = UPPER_AT + STRIPS * EDGE
-CROSS_AT = LOWER_AT + STRIPS // 2 * EDGE
+OFF_AT = {(0, 1): 0, (0, 2): 128, (0, 3): 256, (1, 2): 384, (1, 3): 512, (2, 3): 768}
+UPPER_AT = (640, 704, 896, 960)
+LOWER_AT = (1024, 1088)
+CROSS_AT = 1152
 SUMS_AT = CROSS_AT + TRAITS * STRIPS
 TRAIT_AT = SUMS_AT + STRIPS
-USED = SUMS_AT + 8
+SETS = ((0, 768), (768, 512))
+TOTAL_ROWS = 1280
 CONTRACT_ROWS = (((0,), (0,)), ((), ()))
 CONTRACT_LANES = (((1,), (1,)), ((), ()))
 
 
-def piece_rows(chips):
-    return -(-USED // (2 * chips * 8)) * 8
-
-
 def iota(shape, dim):
     return lax.broadcasted_iota(jnp.int32, shape, dim)
 
@@ -50,7 +47,7 @@
     return sorted(range(1, n), key=lambda d: min(d, n - d))
 
 
-def partial_sums(x_hbm, y_ref, xs, part, top, low, tail, x_sems):
+def loads(x_hbm, xs, x_sems):
     tile = xs.shape[0] // CHUNKS
 
     def chunk(i):
@@ -59,18 +56,39 @@
     def load(i):
         return pltpu.make_async_copy(x_hbm.at[chunk(i)], xs.at[chunk(i)], x_sems.at[i])
 
-    for i in range(CHUNKS):
-        load(i).start()
+    return chunk, load
+
+
+def first_sums(x_hbm, xs, part, top, x_sems):
+    chunk, load = loads(x_hbm, xs, x_sems)
+    half = VARS // 2
     top[...] = jnp.zeros_like(top)
-    low[...] = jnp.zeros_like(low)
-    tail[...] = jnp.zeros_like(tail)
-    half = VARS // 2
 
     def step(i, carry):
         load(i).wait()
         x = xs[chunk(i), :]
+        top[...] += lax.dot_general(x[:, :half], x, CONTRACT_ROWS, preferred_element_type=F32)
+        return carry
+
+    lax.fori_loop(0, CHUNKS, step, 0)
+    for (i, j), at in OFF_AT.items():
+        if i < STRIPS // 2:
+            part[at:at + TILE, :] = top[i * TILE:(i + 1) * TILE, j * TILE:(j + 1) * TILE]
+    for i in range(STRIPS // 2):
+        at, corner = UPPER_AT[i], i * TILE
+        part[at:at + EDGE, :] = top[corner:corner + EDGE, corner:corner + TILE]
+
+
+def second_sums(y_ref, xs, part, top, low, tail):
+    chunk, _ = loads(None, xs, None)
+    tile = xs.shape[0] // CHUNKS
+    half = VARS // 2
+    low[...] = jnp.zeros_like(low)
+    tail[...] = jnp.zeros_like(tail)
+
+    def step(i, carry):
+        x = xs[chunk(i), :]
         lead = jnp.concatenate([y_ref[:, chunk(i)], jnp.ones((TRAITS, tile), BF16)], axis=0)
-        top[...] += lax.dot_general(x[:, :half], x, CONTRACT_ROWS, preferred_element_type=F32)
         low[...] += lax.dot_general(
             x[:, half:], x[:, half:], CONTRACT_ROWS, preferred_element_type=F32
         )
@@ -78,30 +96,21 @@
         return carry
 
     lax.fori_loop(0, CHUNKS, step, 0)
-
-    def tile_of(i, j, first):
-        rows, columns = i * TILE + first, j * TILE
-        source = top
-        if rows >= half:
-            source, rows, columns = low, rows - half, columns - half
-        return source[rows:(i + 1) * TILE - (half if source is low else 0), columns:columns + TILE]
-
-    for at, (i, j) in enumerate(OFF_TILES):
-        part[at * TILE:(at + 1) * TILE, :] = tile_of(i, j, 0)
     left = iota((EDGE, TILE), 1) < EDGE
-    for i in range(STRIPS):
-        at = UPPER_AT + i * EDGE
-        part[at:at + EDGE, :] = tile_of(i, i, 0)[:EDGE]
-    for i in range(STRIPS // 2):
-        at = LOWER_AT + i * EDGE
+    at = OFF_AT[2, 3]
+    part[at:at + TILE, :] = low[:TILE, TILE:]
+    for i in range(2):
+        at, corner = UPPER_AT[2 + i], i * TILE
+        part[at:at + EDGE, :] = low[corner:corner + EDGE, corner:corner + TILE]
+    for at, source in zip(LOWER_AT, (top, low)):
         part[at:at + EDGE, :] = jnp.where(
-            left, pltpu.roll(tile_of(2 * i, 2 * i, EDGE), EDGE, 1),
-            tile_of(2 * i + 1, 2 * i + 1, EDGE),
+            left, pltpu.roll(source[EDGE:TILE, :TILE], EDGE, 1),
+            source[TILE + EDGE:2 * TILE, TILE:2 * TILE],
         )
     for j in range(STRIPS):
         at = CROSS_AT + j * TRAITS
         part[at:at + TRAITS, :] = tail[0:TRAITS, j * TILE:(j + 1) * TILE]
-    part[SUMS_AT:, :] = jnp.zeros((part.shape[0] - SUMS_AT, TILE), F32)
+    part[SUMS_AT:, :] = jnp.zeros((TOTAL_ROWS - SUMS_AT, TILE), F32)
     for j in range(STRIPS):
         part[SUMS_AT + j:SUMS_AT + j + 1, :] = tail[
             TRAITS:TRAITS + 1, j * TILE:(j + 1) * TILE
@@ -132,7 +141,7 @@
     )
 
 
-def people_sum(chips, part, full, half, mine, other_half, ours, slots, sems):
+def people_sum(chips, base, part, full, half, mine, other_half, ours, slots, sems):
     (
         pair_send, pair_recv, near_send, near_recv, spread_send, spread_recv,
         gather_send, gather_recv, near_back_send, near_back_recv, pass_send, pass_recv,
@@ -150,16 +159,18 @@
         return pl.ds(pl.multiple_of(start, 8), count)
 
     pair = remote(
-        part.at[rows_at(other * rows, rows)], half, pair_send, pair_recv, 2 * z + other, b
+        part.at[rows_at(base + other * rows, rows)], half, pair_send, pair_recv, 2 * z + other, b
     )
     pair.start()
+    yield
     pair.wait()
-    mine[...] = part[rows_at(c * rows, rows), :] + half[...]
+    mine[...] = part[rows_at(base + c * rows, rows), :] + half[...]
     swap = remote(
         mine.at[rows_at((1 - odd) * side, side)], other_half,
         near_send, near_recv, 2 * near + c, b,
     )
     swap.start()
+    yield
     swap.wait()
     ours[...] = mine[rows_at(odd * side, side), :] + other_half[...]
     spread = {}
@@ -170,13 +181,14 @@
             spread_send.at[d], spread_recv.at[d], 2 * (2 * to + odd) + c, b,
         )
         spread[d].start()
+    yield
     total = ours[rows_at(place * piece, piece), :]
     for d in near_first(peers):
         spread[d].wait_recv()
         total = total + slots[d]
 
     def own(parity, at):
-        return rows_at(c * rows + parity * side + at * piece, piece)
+        return rows_at(base + c * rows + parity * side + at * piece, piece)
 
     full[own(odd, place), :] = total
     here = own(odd, place)
@@ -187,6 +199,7 @@
             full.at[here], full.at[here], gather_send.at[d], gather_recv.at[d], to, b
         )
         gather[d].start()
+    yield
     back, passed = {}, {}
     for d in [0] + near_first(peers):
         if d:
@@ -201,6 +214,7 @@
             full.at[here], full.at[here], pass_send.at[d], pass_recv.at[d], 2 * z + other, b
         )
         passed[d].start()
+    yield
     near_place = lax.div(near, 2)
     for d in [0] + near_first(peers):
         back[d].wait_recv()
@@ -210,6 +224,7 @@
             2 * z + other, b,
         )
         passed[peers + d].start()
+    yield
     for copy in passed.values():
         copy.wait()
     for d in range(peers):
@@ -251,14 +266,14 @@
 
 
 def solve(headcount, full, factors_ref, xs, pred, gram, high, low, basis, rows_scr):
-    for at, (i, j) in enumerate(OFF_TILES):
-        tile = full[at * TILE:(at + 1) * TILE, :]
+    for (i, j), at in OFF_AT.items():
+        tile = full[at:at + TILE, :]
         gram[i * TILE:(i + 1) * TILE, j * TILE:(j + 1) * TILE] = tile
         gram[j * TILE:(j + 1) * TILE, i * TILE:(i + 1) * TILE] = tile.T
     left = iota((EDGE, TILE), 1) < EDGE
     for i in range(STRIPS):
-        upper = full[UPPER_AT + i * EDGE:UPPER_AT + (i + 1) * EDGE, :]
-        at = LOWER_AT + i // 2 * EDGE
+        upper = full[UPPER_AT[i]:UPPER_AT[i] + EDGE, :]
+        at = LOWER_AT[i // 2]
         lower = full[at:at + EDGE, :]
         if i % 2 == 0:
             lower = pltpu.roll(lower, EDGE, 1)
@@ -348,11 +363,15 @@
 
 def whole_kernel(
     chips, blocks, headcount, y_ref, factors_ref, x_hbm, ridge_ref, final_ref,
-    xs, part, top, low, tail, full, half, mine, other_half, ours, slots,
-    gram_scr, high, low_part, basis, rows_scr, pred, recv, stacked,
-    packed, last_half, last_mine, last_slots, final,
-    x_sems, *sems,
+    xs, part, top, low, tail, full, *rest,
 ):
+    buffers, rest = (rest[0:5], rest[5:10]), rest[10:]
+    gram_scr, high, low_part, basis, rows_scr, pred, recv, stacked = rest[:8]
+    packed, last_half, last_mine, last_slots, final, x_sems = rest[8:14]
+    sems = rest[14:]
+    _, load = loads(x_hbm, xs, x_sems)
+    for i in range(CHUNKS):
+        load(i).start()
     z, c, b = position()
     person = 2 * z + c
     other = 1 - c
@@ -362,17 +381,26 @@
     for d in range(1, blocks):
         signal(person, lax.rem(b + d, blocks))
 
-    partial_sums(x_hbm, y_ref, xs, part, top, low, tail, x_sems)
+    first_sums(x_hbm, xs, part, top, x_sems)
+    pl.semaphore_wait(pltpu.get_barrier_semaphore(), blocks + chips - 1)
+    stages = [
+        people_sum(chips, base, part, full, *buffers[at], sems[12 * at:12 * at + 12])
+        for at, (base, _) in enumerate(SETS)
+    ]
+    next(stages[0])
+    second_sums(y_ref, xs, part, top, low, tail)
     stacked[...] = jnp.zeros_like(stacked)
-    pl.semaphore_wait(pltpu.get_barrier_semaphore(), blocks + chips - 1)
-    people_sum(chips, part, full, half, mine, other_half, ours, slots, sems[:12])
+    next(stages[1])
+    for _ in range(6):
+        for stage in stages:
+            next(stage, None)
     factors, radius = solve(
         headcount, full, factors_ref, xs, pred, gram_scr, high, low_part, basis, rows_scr
     )
 
     (
         move_send, move_recv, pair_send, pair_recv, spread_send, spread_recv, pass_send, pass_recv,
-    ) = sems[12:]
+    ) = sems[24:]
     moves = {}
     for d in range(1, blocks):
         to = lax.rem(b + d, blocks)
@@ -488,9 +516,6 @@
 def per_device(chips, blocks, x, y, factors):
     people = x.shape[0]
     headcount = float(people * chips * 2)
-    piece = piece_rows(chips)
-    total_rows = 2 * chips * piece
-    core_rows = chips * piece
     peers = chips // 2
     half = VARS // 2
     width = people // PARTS
@@ -508,16 +533,19 @@
         out_shape=[rows_shape, jax.ShapeDtypeStruct((rows, TILE), F32)],
         scratch_shapes=[
             pltpu.VMEM((people, VARS), BF16),
-            pltpu.VMEM((total_rows, TILE), F32),
+            pltpu.VMEM((TOTAL_ROWS, TILE), F32),
             pltpu.VMEM((half, VARS), F32),
             pltpu.VMEM((half, half), F32),
             pltpu.VMEM((2 * TRAITS, VARS), F32),
-            pltpu.VMEM((total_rows, TILE), F32),
-            pltpu.VMEM((core_rows, TILE), F32),
-            pltpu.VMEM((core_rows, TILE), F32),
-            pltpu.VMEM((core_rows // 2, TILE), F32),
-            pltpu.VMEM((core_rows // 2, TILE), F32),
-            pltpu.VMEM((peers, piece, TILE), F32),
+            pltpu.VMEM((TOTAL_ROWS, TILE), F32),
+            *(
+                pltpu.VMEM(shape, F32)
+                for _, count in SETS
+                for shape in (
+                    (count // 2, TILE), (count // 2, TILE), (count // 4, TILE), (count // 4, TILE),
+                    (peers, count // (2 * chips), TILE),
+                )
+            ),
             pltpu.VMEM((VARS, VARS), F32),
             pltpu.VMEM((VARS, VARS), BF16),
             pltpu.VMEM((VARS, VARS), BF16),
@@ -532,8 +560,11 @@
             pltpu.VMEM((chips, rows // 2, TILE), F32),
             pltpu.VMEM((rows, TILE), F32),
             DMA((CHUNKS,)),
-            DMA, DMA, DMA, DMA, DMA((peers,)), DMA((peers,)), DMA((peers,)), DMA((peers,)),
-            DMA((peers,)), DMA((peers,)), DMA((chips,)), DMA((chips,)),
+            *(
+                DMA(shape)
+                for _ in SETS
+                for shape in 4 * [()] + 6 * [(peers,)] + 2 * [(chips,)]
+            ),
             DMA((blocks,)), DMA((blocks,)), DMA, DMA, DMA((chips,)), DMA((chips,)), DMA, DMA,
         ],
         compiler_params=pltpu.CompilerParams(collective_id=0, has_side_effects=True),

time: 82.8 us -> 81.5 us (0.984)
  Pallas kernels: 81.8 us -> 80.7 us
    pallas_call x1, Pallas kernels: 80.1 us -> 79 us  [per_device(): pl.pallas_call(functools.partial(whole_kernel, chips, blocks, headcount),...]
where the time goes in v3:
time: 81.5 us; the launch traced here: 81.3 us
  Pallas kernels  80.7 us (99%)
    pallas_call x1, Pallas kernels, per_device(): pl.pallas_call(functools.partial(whole_kernel, chips, blocks, headcount),...  79 us
    pallas_call x1, Pallas kernels, per_device(): pl.pallas_call(functools.partial(finish_kernel, size, headcount), in_spec...  1.69 us

profile of v3, /device:TPU:1, one launch (start us, length us, event | category | flops | bytes accessed | tf_op | source)
XLA Modules:
  0.0 81.3 jit_solution(18054756625310765138)
XLA Ops:
  0.6 79.0 %whole.1 = (f32[80,512]{1,0:T(8,128)}, f32[48,128]{1,0:T(8,128)}) custom-call(bf16[16,4096]{1,0:T(8,128)(2,1)} %bitcast.2, f32[5]{0:T(128)} %factors_ref.1, bf16[4096,512]{1,0:T(8,128)(2,1)} %x_hbm.1), custom_call_target="tpu_custom_call" | custom-call | tf_op jit(solution)/shard_map/whole/pallas_call | solution.py:525
  79.6 1.7 %finish.1 = (f32[80,512]{1,0:T(8,128)}, f32[1,80,80]{2,1,0:T(8,128)}, f32[1,80]{1,0:T(1,128)}) custom-call(f32[80,512]{1,0:T(8,128)} %get-tuple-element.8.rows_ref, f32[48,128]{1,0:T(8,128)} %get-tuple-element.9.flat_ref), custom_call_target="tpu_custom_call" | custom-call | tf_op jit(solution)/shard_map/finish/pallas_call | solution.py:573

commit v4 on v3

--- a/solution.py
+++ b/solution.py
@@ -436,17 +436,18 @@
     gram = lax.dot_general(w, w, CONTRACT_LANES, preferred_element_type=F32)
 
     size = blocks * LAMBDAS
-    part = size // 2
+    side = size // 2
+    group = packed.shape[0] * packed.shape[1]
     square = (TILE, TILE)
     row, lane = iota(square, 0), iota(square, 1)
-    cols_a = ((lane < size) & (row == slot_of(lane))) | ((lane == 120) & (row == LAMBDAS))
-    cols_b = (
-        (lane >= size) & (lane < size + part) & (row == slot_of(lane - part))
-    ) | ((lane == 121) & (row == LAMBDAS))
-    strip = (packed.shape[0], TILE)
-    row, lane = iota(strip, 0), iota(strip, 1)
-    rows_a = (row < part) & (lane == slot_of(row))
-    rows_b = (row < part) & (lane == slot_of(row + part))
+    cols_a = (lane < side) & (row == slot_of(lane))
+    cols_b = (lane < side) & (row == slot_of(lane + side))
+    tall = (88, TILE)
+    row, lane = iota(tall, 0), iota(tall, 1)
+    rows_a = ((row < size) & (lane == slot_of(row))) | ((row == size + 1) & (lane == LAMBDAS))
+    rows_b = ((row < side) & (lane == slot_of(row + side))) | (
+        (row == size + 2) & (lane == LAMBDAS)
+    )
 
     def select(left, right):
         inner = jnp.dot(
@@ -456,17 +457,23 @@
             left.astype(F32), inner, precision=HIGHEST, preferred_element_type=F32
         )
 
-    packed[...] = select(rows_a, cols_a) + select(rows_b, cols_b)
-
-    rows = packed.shape[0] // 2
-
-    def side(core):
-        return pl.ds(pl.multiple_of(core * rows, 8), rows)
-
-    pair = remote(packed.at[side(other)], last_half, pair_send, pair_recv, 2 * z + other, b)
+    form, second = select(rows_a, cols_a), select(rows_b, cols_b)
+    diagonal = jnp.sum(
+        jnp.where((row == lane) & (row < side), second, 0.0), axis=0, keepdims=True
+    )
+    form = jnp.where(((row < side) & (row > lane)) | (row == size + 2), second, form)
+    form = jnp.where(row == size, diagonal, form)
+    flat = form[0:group] + (
+        pltpu.roll(form[group:2 * group], side, 1)
+        + pltpu.roll(form[2 * group:3 * group], 2 * side, 1)
+    )
+    packed[0] = flat[:group // 2]
+    packed[1] = flat[group // 2:]
+
+    pair = remote(packed.at[other], last_half, pair_send, pair_recv, 2 * z + other, b)
     pair.start()
     pair.wait()
-    last_mine[...] = packed[side(c), :] + last_half[...]
+    last_mine[...] = packed[c] + last_half[...]
     spread = {}
     for d in far_first(chips):
         spread[d] = remote(
@@ -480,8 +487,8 @@
     total = last_slots[0]
     for chip in range(1, chips):
         total = total + last_slots[chip]
-    final[side(c), :] = total
-    passed = remote(final.at[side(c)], final.at[side(c)], pass_send, pass_recv, 2 * z + other, b)
+    final[c] = total
+    passed = remote(final.at[c], final.at[c], pass_send, pass_recv, 2 * z + other, b)
     passed.start()
     passed.wait()
     for d in range(1, chips):
@@ -492,21 +499,38 @@
     final_ref[...] = final[...]
 
 
-def finish_kernel(size, headcount, rows_ref, flat_ref, ridge_ref, gram_ref, cross_ref):
+def finish_kernel(size, headcount, rows_ref, flat_ref, ridge_ref, gram_ref, cross_ref, form):
     ridge_ref[...] = rows_ref[...]
-    part = size // 2
-    flat = flat_ref[...]
-    turned = jnp.concatenate(
-        [flat, jnp.zeros((TILE - flat.shape[0], TILE), F32)], axis=0
-    ).T
-    shifted = pltpu.roll(flat, TILE - part, 1)
-    lane = iota((part, TILE), 1)
-    lower = jnp.where(lane < part, turned[part:size, :], shifted[:part, :])
-    gram_ref[0, 0:part, :] = flat[:part, :size] * (1.0 / headcount)
-    gram_ref[0, part:size, :] = lower[:, :size] * (1.0 / headcount)
-    lane = iota((1, TILE), 1)
-    pair_row = jnp.where(lane < part, turned[120:121, :], pltpu.roll(turned[121:122, :], part, 1))
-    cross_ref[...] = pair_row[:, :size] * (1.0 / math.sqrt(headcount))
+    side = size // 2
+    half = flat_ref.shape[1]
+    for which in range(3):
+        for core in range(2):
+            at = (2 * which + core) * half
+            values = flat_ref[core]
+            form[at:at + half, :] = (
+                pltpu.roll(values, TILE - which * side, 1) if which else values
+            )
+
+    def turn(values):
+        padding = jnp.zeros((TILE - values.shape[0], TILE), F32)
+        return jnp.concatenate([values, padding], axis=0).T
+
+    mixed, corner = form[0:side, :], form[side:size, :]
+    mixed_turned = turn(mixed)[:side, :]
+    row, lane = iota((side, TILE), 0), iota((side, TILE), 1)
+    first = jnp.where(row <= lane, mixed, mixed_turned)
+    last = jnp.where(row > lane, mixed, mixed_turned)
+    last = jnp.where(row == lane, form[size:size + 1, :], last)
+    near = lane < side
+    upper = jnp.where(near, first, pltpu.roll(turn(corner)[:side, :], side, 1))
+    lower = jnp.where(near, corner, pltpu.roll(last, side, 1))
+    gram_ref[0, 0:side, :] = upper[:, :size] * (1.0 / headcount)
+    gram_ref[0, side:size, :] = lower[:, :size] * (1.0 / headcount)
+    cross = jnp.where(
+        iota((1, TILE), 1) < side, form[size + 1:size + 2, :],
+        pltpu.roll(form[size + 2:size + 3, :], side, 1),
+    )
+    cross_ref[...] = cross[:, :size] * (1.0 / math.sqrt(headcount))
 
 
 VMEM = pl.BlockSpec(memory_space=pltpu.VMEM)
@@ -520,7 +544,7 @@
     half = VARS // 2
     width = people // PARTS
     size = blocks * LAMBDAS
-    rows = 48
+    half_rows = 14
     rows_shape = jax.ShapeDtypeStruct((TRAITS * LAMBDAS, VARS), F32)
     ridge, final = pl.pallas_call(
         functools.partial(whole_kernel, chips, blocks, headcount),
@@ -530,7 +554,7 @@
             pl.BlockSpec(memory_space=pl.ANY),
         ],
         out_specs=[VMEM, VMEM],
-        out_shape=[rows_shape, jax.ShapeDtypeStruct((rows, TILE), F32)],
+        out_shape=[rows_shape, jax.ShapeDtypeStruct((2, half_rows, TILE), F32)],
         scratch_shapes=[
             pltpu.VMEM((people, VARS), BF16),
             pltpu.VMEM((TOTAL_ROWS, TILE), F32),
@@ -554,11 +578,11 @@
             pltpu.VMEM((TRAITS, PARTS * LAMBDAS, width), BF16),
             pltpu.VMEM((blocks, PARTS * LAMBDAS, width), BF16),
             pltpu.VMEM((blocks * SLOT, people), F32),
-            pltpu.VMEM((rows, TILE), F32),
-            pltpu.VMEM((rows // 2, TILE), F32),
-            pltpu.VMEM((rows // 2, TILE), F32),
-            pltpu.VMEM((chips, rows // 2, TILE), F32),
-            pltpu.VMEM((rows, TILE), F32),
+            pltpu.VMEM((2, half_rows, TILE), F32),
+            pltpu.VMEM((half_rows, TILE), F32),
+            pltpu.VMEM((half_rows, TILE), F32),
+            pltpu.VMEM((chips, half_rows, TILE), F32),
+            pltpu.VMEM((2, half_rows, TILE), F32),
             DMA((CHUNKS,)),
             *(
                 DMA(shape)
@@ -579,6 +603,7 @@
             jax.ShapeDtypeStruct((1, size, size), F32),
             jax.ShapeDtypeStruct((1, size), F32),
         ],
+        scratch_shapes=[pltpu.VMEM((88, TILE), F32)],
         name="finish",
     )(ridge, final)
     return ridge.T, gram, cross

time: 81.5 us -> 78.8 us (0.967)
  Pallas kernels: 80.7 us -> 78 us
    pallas_call x1, Pallas kernels: 79 us -> 76.2 us  [per_device(): pl.pallas_call(functools.partial(whole_kernel, chips, blocks, headcount),...]
where the time goes in v4:
time: 78.8 us; the launch traced here: 78.6 us
  Pallas kernels  78 us (99%)
    pallas_call x1, Pallas kernels, per_device(): pl.pallas_call(functools.partial(whole_kernel, chips, blocks, headcount),...  76.2 us
    pallas_call x1, Pallas kernels, per_device(): pl.pallas_call(functools.partial(finish_kernel, size, headcount), in_spec...  1.76 us

profile of v4, /device:TPU:1, one launch (start us, length us, event | category | flops | bytes accessed | tf_op | source)
XLA Modules:
  0.0 78.6 jit_solution(10969711656430349573)
XLA Ops:
  0.6 76.2 %whole.1 = (f32[80,512]{1,0:T(8,128)}, f32[2,14,128]{2,1,0:T(8,128)}) custom-call(bf16[16,4096]{1,0:T(8,128)(2,1)} %bitcast.2, f32[5]{0:T(128)} %factors_ref.1, bf16[4096,512]{1,0:T(8,128)(2,1)} %x_hbm.1), custom_call_target="tpu_custom_call" | custom-call | tf_op jit(solution)/shard_map/whole/pallas_call | solution.py:549
  76.9 1.8 %finish.1 = (f32[80,512]{1,0:T(8,128)}, f32[1,80,80]{2,1,0:T(8,128)}, f32[1,80]{1,0:T(1,128)}) custom-call(f32[80,512]{1,0:T(8,128)} %get-tuple-element.8.rows_ref, f32[2,14,128]{2,1,0:T(8,128)} %get-tuple-element.9.flat_ref), custom_call_target="tpu_custom_call" | custom-call | tf_op jit(solution)/shard_map/finish/pallas_call | solution.py:597

commit v5 on v4

--- a/solution.py
+++ b/solution.py
@@ -173,17 +173,40 @@
     yield
     swap.wait()
     ours[...] = mine[rows_at(odd * side, side), :] + other_half[...]
+    turn = 2 - 4 * c
+
+    def at_place(step):
+        return lax.rem(place + step + 2 * peers, peers)
+
+    def person_at(step):
+        return 2 * (2 * at_place(step) + odd) + c
+
+    def rows_for(step):
+        return rows_at(at_place(step) * piece, piece)
+
     spread = {}
-    for d in far_first(peers):
-        to = lax.rem(place + d, peers)
+
+    def send_piece(d, step, to):
         spread[d] = remote(
-            ours.at[rows_at(to * piece, piece)], slots.at[d],
-            spread_send.at[d], spread_recv.at[d], 2 * (2 * to + odd) + c, b,
+            ours.at[rows_for(step)], slots.at[d], spread_send.at[d], spread_recv.at[d],
+            person_at(to), b,
         )
         spread[d].start()
-    yield
-    total = ours[rows_at(place * piece, piece), :]
-    for d in near_first(peers):
+
+    send_piece(4, 4, turn)
+    send_piece(3, 3, 1)
+    send_piece(5, -3, -1)
+    send_piece(1, 1, 1)
+    send_piece(7, -1, -1)
+    yield
+    for d, step in ((3, 2), (5, -2), (4, turn)):
+        spread[d].wait_recv()
+        ours[rows_for(step), :] = ours[rows_for(step), :] + slots[d]
+    send_piece(2, 2, 2)
+    send_piece(6, -2, -2)
+    yield
+    total = ours[rows_for(0), :]
+    for d in (1, 7, 2, 6):
         spread[d].wait_recv()
         total = total + slots[d]
 
@@ -191,20 +214,25 @@
         return rows_at(base + c * rows + parity * side + at * piece, piece)
 
     full[own(odd, place), :] = total
-    here = own(odd, place)
     gather = {}
-    for d in far_first(peers):
-        to = 2 * (2 * lax.rem(place + d, peers) + odd) + c
+
+    def hand_on(d, step, to):
+        rows_here = own(odd, at_place(step))
         gather[d] = remote(
-            full.at[here], full.at[here], gather_send.at[d], gather_recv.at[d], to, b
+            full.at[rows_here], full.at[rows_here], gather_send.at[d], gather_recv.at[d],
+            person_at(to), b,
         )
         gather[d].start()
+
+    hand_on(2, 0, 2)
+    hand_on(6, 0, -2)
+    hand_on(1, 0, 1)
+    hand_on(7, 0, -1)
     yield
     back, passed = {}, {}
-    for d in [0] + near_first(peers):
-        if d:
-            gather[d].wait_recv()
-        here = own(odd, lax.rem(place + peers - d, peers))
+
+    def share(d):
+        here = own(odd, at_place(-d))
         back[d] = remote(
             full.at[here], full.at[here], near_back_send.at[d], near_back_recv.at[d],
             2 * near + c, b,
@@ -214,9 +242,25 @@
             full.at[here], full.at[here], pass_send.at[d], pass_recv.at[d], 2 * z + other, b
         )
         passed[d].start()
+
+    share(0)
+    gather[2].wait_recv()
+    hand_on(3, -2, 1)
+    gather[6].wait_recv()
+    hand_on(5, 2, -1)
+    hand_on(4, -turn, turn)
+    for d in (1, 7):
+        gather[d].wait_recv()
+        share(d)
+    share(2)
+    share(6)
+    yield
+    for d in (3, 5, 4):
+        gather[d].wait_recv()
+        share(d)
     yield
     near_place = lax.div(near, 2)
-    for d in [0] + near_first(peers):
+    for d in (0, 1, 7, 2, 6, 3, 5, 4):
         back[d].wait_recv()
         here = own(1 - odd, lax.rem(near_place + peers - d, peers))
         passed[peers + d] = remote(
@@ -391,7 +435,7 @@
     second_sums(y_ref, xs, part, top, low, tail)
     stacked[...] = jnp.zeros_like(stacked)
     next(stages[1])
-    for _ in range(6):
+    for _ in range(8):
         for stage in stages:
             next(stage, None)
     factors, radius = solve(

time: 78.8 us -> 81.5 us (1.034)
  Pallas kernels: 78 us -> 80.7 us
    pallas_call x1, Pallas kernels: 76.2 us -> 79 us  [per_device(): pl.pallas_call(functools.partial(whole_kernel, chips, blocks, headcount),...]
where the time goes in v5:
time: 81.5 us; the launch traced here: 81.4 us
  Pallas kernels  80.7 us (99%)
    pallas_call x1, Pallas kernels, per_device(): pl.pallas_call(functools.partial(whole_kernel, chips, blocks, headcount),...  79 us
    pallas_call x1, Pallas kernels, per_device(): pl.pallas_call(functools.partial(finish_kernel, size, headcount), in_spec...  1.76 us

profile of v5, /device:TPU:1, one launch (start us, length us, event | category | flops | bytes accessed | tf_op | source)
XLA Modules:
  0.0 81.4 jit_solution(5889179257523816798)
XLA Ops:
  0.6 79.0 %whole.1 = (f32[80,512]{1,0:T(8,128)}, f32[2,14,128]{2,1,0:T(8,128)}) custom-call(bf16[16,4096]{1,0:T(8,128)(2,1)} %bitcast.2, f32[5]{0:T(128)} %factors_ref.1, bf16[4096,512]{1,0:T(8,128)(2,1)} %x_hbm.1), custom_call_target="tpu_custom_call" | custom-call | tf_op jit(solution)/shard_map/whole/pallas_call | solution.py:593
  79.6 1.8 %finish.1 = (f32[80,512]{1,0:T(8,128)}, f32[1,80,80]{2,1,0:T(8,128)}, f32[1,80]{1,0:T(1,128)}) custom-call(f32[80,512]{1,0:T(8,128)} %get-tuple-element.8.rows_ref, f32[2,14,128]{2,1,0:T(8,128)} %get-tuple-element.9.flat_ref), custom_call_target="tpu_custom_call" | custom-call | tf_op jit(solution)/shard_map/finish/pallas_call | solution.py:641

commit v6 on v4

--- a/solution.py
+++ b/solution.py
@@ -356,22 +356,40 @@
     return factors, radius
 
 
+def grid_hops(d, blocks):
+    edge = math.isqrt(blocks)
+    return sum(min(step, edge - step) for step in divmod(d, edge))
+
+
+def grid_shift(b, d, sign, blocks):
+    edge = math.isqrt(blocks)
+    dx, dy = divmod(d, edge)
+    x = lax.rem(lax.div(b, edge) + edge + sign * dx, edge)
+    y = lax.rem(lax.rem(b, edge) + edge + sign * dy, edge)
+    return x * edge + y
+
+
 def slot_of(compact):
     block = lax.shift_right_logical(compact * 205, 10)
     return block * SLOT + (compact - block * LAMBDAS)
 
 
 def whole_kernel(
-    chips, blocks, headcount, y_ref, factors_ref, x_hbm, ridge_ref, final_ref,
+    chips, blocks, headcount, y_hbm, factors_hbm, x_hbm, ridge_ref, final_ref,
     xs, part, top, low, tail, full, *rest,
 ):
     buffers, rest = (rest[0:5], rest[5:10]), rest[10:]
     gram_scr, high, low_part, basis, rows_scr, pred, recv, stacked = rest[:8]
     packed, last_half, last_mine, last_slots, final, x_sems = rest[8:14]
-    sems = rest[14:]
+    y_ref, factors_ref, y_sem, factors_sem = rest[14:18]
+    sems = rest[18:]
     _, load = loads(x_hbm, xs, x_sems)
     for i in range(CHUNKS):
         load(i).start()
+    y_load = pltpu.make_async_copy(y_hbm, y_ref, y_sem)
+    y_load.start()
+    factors_load = pltpu.make_async_copy(factors_hbm, factors_ref, factors_sem)
+    factors_load.start()
     z, c, b = position()
     person = 2 * z + c
     other = 1 - c
@@ -388,6 +406,8 @@
         for at, (base, _) in enumerate(SETS)
     ]
     next(stages[0])
+    y_load.wait()
+    factors_load.wait()
     second_sums(y_ref, xs, part, top, low, tail)
     stacked[...] = jnp.zeros_like(stacked)
     next(stages[1])
@@ -402,8 +422,9 @@
         move_send, move_recv, pair_send, pair_recv, spread_send, spread_recv, pass_send, pass_recv,
     ) = sems[24:]
     moves = {}
-    for d in range(1, blocks):
-        to = lax.rem(b + d, blocks)
+    steps = sorted(range(1, blocks), key=lambda d: grid_hops(d, blocks))
+    for d in reversed(steps):
+        to = grid_shift(b, d, 1, blocks)
         moves[d] = remote(
             pred.at[to], recv.at[d], move_send.at[d], move_recv.at[d], person, to
         )
@@ -427,9 +448,9 @@
             ]
 
     place(b, pred[b])
-    for d in range(1, blocks):
+    for d in steps:
         moves[d].wait_recv()
-        place(lax.rem(b + blocks - d, blocks), recv[d])
+        place(grid_shift(b, d, -1, blocks), recv[d])
     stacked[LAMBDAS:LAMBDAS + 1, :] = trait_row[LAMBDAS:LAMBDAS + 1, :]
 
     w = stacked[...].astype(BF16)
@@ -549,8 +570,8 @@
     ridge, final = pl.pallas_call(
         functools.partial(whole_kernel, chips, blocks, headcount),
         in_specs=[
-            VMEM,
-            pl.BlockSpec(memory_space=pltpu.SMEM),
+            pl.BlockSpec(memory_space=pl.ANY),
+            pl.BlockSpec(memory_space=pl.ANY),
             pl.BlockSpec(memory_space=pl.ANY),
         ],
         out_specs=[VMEM, VMEM],
@@ -584,6 +605,9 @@
             pltpu.VMEM((chips, half_rows, TILE), F32),
             pltpu.VMEM((2, half_rows, TILE), F32),
             DMA((CHUNKS,)),
+            pltpu.VMEM((TRAITS, people), BF16),
+            pltpu.SMEM((LAMBDAS,), F32),
+            DMA, DMA,
             *(
                 DMA(shape)
                 for _ in SETS

time: 78.8 us -> 78.6 us (level)
  no operation moved by 1% of the time
where the time goes in v6:
time: 78.6 us; the launch traced here: 78.4 us
  Pallas kernels  77.8 us (99%)
    pallas_call x1, Pallas kernels, per_device(): pl.pallas_call(functools.partial(whole_kernel, chips, blocks, headcount),...  76 us
    pallas_call x1, Pallas kernels, per_device(): pl.pallas_call(functools.partial(finish_kernel, size, headcount), in_spec...  1.76 us

profile of v6, /device:TPU:1, one launch (start us, length us, event | category | flops | bytes accessed | tf_op | source)
XLA Modules:
  0.0 78.4 jit_solution(17268794918626724427)
XLA Ops:
  0.6 76.0 %whole.1 = (f32[80,512]{1,0:T(8,128)}, f32[2,14,128]{2,1,0:T(8,128)}) custom-call(bf16[16,4096]{1,0:T(8,128)(2,1)} %bitcast.2, f32[5]{0:T(128)} %factors_hbm.1, bf16[4096,512]{1,0:T(8,128)(2,1)} %x_hbm.1), custom_call_target="tpu_custom_call" | custom-call | tf_op jit(solution)/shard_map/whole/pallas_call | solution.py:570
  76.7 1.8 %finish.1 = (f32[80,512]{1,0:T(8,128)}, f32[1,80,80]{2,1,0:T(8,128)}, f32[1,80]{1,0:T(1,128)}) custom-call(f32[80,512]{1,0:T(8,128)} %get-tuple-element.8.rows_ref, f32[2,14,128]{2,1,0:T(8,128)} %get-tuple-element.9.flat_ref), custom_call_target="tpu_custom_call" | custom-call | tf_op jit(solution)/shard_map/finish/pallas_call | solution.py:621

commit v7 on v6

--- a/solution.py
+++ b/solution.py
@@ -199,7 +199,6 @@
             full.at[here], full.at[here], gather_send.at[d], gather_recv.at[d], to, b
         )
         gather[d].start()
-    yield
     back, passed = {}, {}
     for d in [0] + near_first(peers):
         if d:
@@ -214,7 +213,7 @@
             full.at[here], full.at[here], pass_send.at[d], pass_recv.at[d], 2 * z + other, b
         )
         passed[d].start()
-    yield
+        yield
     near_place = lax.div(near, 2)
     for d in [0] + near_first(peers):
         back[d].wait_recv()
@@ -224,7 +223,7 @@
             2 * z + other, b,
         )
         passed[peers + d].start()
-    yield
+        yield
     for copy in passed.values():
         copy.wait()
     for d in range(peers):
@@ -411,7 +410,7 @@
     second_sums(y_ref, xs, part, top, low, tail)
     stacked[...] = jnp.zeros_like(stacked)
     next(stages[1])
-    for _ in range(6):
+    for _ in range(32):
         for stage in stages:
             next(stage, None)
     factors, radius = solve(

time: 78.6 us -> 79 us (level)
  no operation moved by 1% of the time
where the time goes in v7:
time: 79 us; the launch traced here: 78.9 us
  Pallas kernels  78.2 us (99%)
    pallas_call x1, Pallas kernels, per_device(): pl.pallas_call(functools.partial(whole_kernel, chips, blocks, headcount),...  76.5 us
    pallas_call x1, Pallas kernels, per_device(): pl.pallas_call(functools.partial(finish_kernel, size, headcount), in_spec...  1.76 us

profile of v7, /device:TPU:1, one launch (start us, length us, event | category | flops | bytes accessed | tf_op | source)
XLA Modules:
  0.0 78.9 jit_solution(17311159435139463104)
XLA Ops:
  0.6 76.5 %whole.1 = (f32[80,512]{1,0:T(8,128)}, f32[2,14,128]{2,1,0:T(8,128)}) custom-call(bf16[16,4096]{1,0:T(8,128)(2,1)} %bitcast.2, f32[5]{0:T(128)} %factors_hbm.1, bf16[4096,512]{1,0:T(8,128)(2,1)} %x_hbm.1), custom_call_target="tpu_custom_call" | custom-call | tf_op jit(solution)/shard_map/whole/pallas_call | solution.py:569
  77.1 1.8 %finish.1 = (f32[80,512]{1,0:T(8,128)}, f32[1,80,80]{2,1,0:T(8,128)}, f32[1,80]{1,0:T(1,128)}) custom-call(f32[80,512]{1,0:T(8,128)} %get-tuple-element.8.rows_ref, f32[2,14,128]{2,1,0:T(8,128)} %get-tuple-element.9.flat_ref), custom_call_target="tpu_custom_call" | custom-call | tf_op jit(solution)/shard_map/finish/pallas_call | solution.py:620
